TPU v7x, 32 devices: a whole 2x2x4 slice. The times are simulated.
32 devices in a mesh: sec: 8 (over z, x), row: 4 (over y, core).
Axes of the slice: x: 2, y: 2, z: 4, core: 2. Of those that a mesh axis runs over, the one named last changes fastest.
Arguments:
- left_block: bfloat16 [16, 2048, 128], P('sec', 'row'), may hold values from -6 to 6
- right_block: bfloat16 [16, 128, 2048], P('sec'), may hold values from -6 to 6
- left_ops: float32 [4, 16, 16], replicated, may hold values from -1.5 to 1.5
- right_ops: float32 [4, 16, 16], replicated, may hold values from -1.5 to 1.5
- charges: int32 [16], replicated, may hold values from 0 to 6
- live_states: int32 [16], replicated, may hold values from 64 to 128
- kept: int32 [16], replicated, may hold values from 64 to 128
- start: int32 [16, 128], replicated, may hold values from 0 to 511, all different within a row
Outputs:
- basis: float32 [16, 2048, 128], P('sec', 'row')
- right_new: float32 [16, 128, 2048], P('sec', None, 'row')
Inputs may be any that keep to these rules, and one draw needn't show every extreme that they name: The 128 start columns of a sector are distinct.
All inputs are finite; a program needn't handle non-finite values.
Results may differ from a plain program's by a relative error of at most 0.0065.
Values may be sent and summed in bfloat16 or wider, within the bound.
A program may use at most 64 MiB of HBM per device.

v0:
```python
import functools

import jax
import jax.numpy as jnp
from jax import lax
from jax.experimental import pallas as pl
from jax.experimental.pallas import tpu as pltpu
from jax.sharding import PartitionSpec as P

MESH = pl.DeviceIdType.MESH
HIGHEST = lax.Precision.HIGHEST
F32, BF16 = jnp.float32, jnp.bfloat16
chemical = 0.4
ITERS = 2
PANEL = 16
CHUNKS = 2
VM = pl.BlockSpec(memory_space=pltpu.VMEM)
SM = pl.BlockSpec(memory_space=pltpu.SMEM)


def nn(a, b, precision=None):
    return lax.dot_general(
        a, b, (((1,), (0,)), ((), ())), precision=precision, preferred_element_type=F32
    )


def nt(a, b, precision=None):
    return lax.dot_general(
        a, b, (((1,), (1,)), ((), ())), precision=precision, preferred_element_type=F32
    )


def tn(a, b, precision=None):
    return lax.dot_general(
        a, b, (((0,), (0,)), ((), ())), precision=precision, preferred_element_type=F32
    )


def split2(x):
    high = x.astype(BF16)
    return high, (x - high.astype(F32)).astype(BF16)


def split3(x):
    high, rest = x.astype(BF16), None
    rest = x - high.astype(F32)
    mid = rest.astype(BF16)
    return high, mid, (rest - mid.astype(F32)).astype(BF16)


def presplit_nn(parts, x):
    high, low = split2(x)
    both = nn(parts[0], jnp.concatenate([high, low], axis=1))
    width = x.shape[1]
    return both[:, :width] + both[:, width:] + nn(parts[1], high)


def nt3(a, b):
    ah, al = split2(a)
    bh, bl = split2(b)
    return nt(jnp.concatenate([ah, al, ah], axis=1), jnp.concatenate([bh, bh, bl], axis=1))


def iota(shape, dim):
    return lax.broadcasted_iota(jnp.int32, shape, dim)


def exchange_kernel(row_count, mask, left_ref, right_ref, left_out, right_out, send, recv):
    row, sec = lax.axis_index("row"), lax.axis_index("sec")
    rows = left_ref.shape[1]
    depth = right_ref.shape[1] // row_count

    def peer_row(distance):
        return (sec, jnp.bitwise_xor(row, distance))

    partner = (jnp.bitwise_xor(sec, mask), row)
    distances = []
    step = row_count // 2
    while step:
        distances.append(step)
        step //= 2
    barrier = pltpu.get_barrier_semaphore()
    for device in [partner] + [peer_row(d) for d in distances]:
        pl.semaphore_signal(barrier, inc=1, device_id=device, device_id_type=MESH)
    pl.semaphore_wait(barrier, 1 + len(distances))

    def left_at(owner):
        return left_out.at[:, pl.ds(pl.multiple_of(owner * rows, rows), rows), :]

    def right_at(ref, owner, c):
        size = depth // CHUNKS
        return ref.at[:, pl.ds(pl.multiple_of(owner * depth + c * size, size), size), :]

    copies = []

    def go(source, target, device):
        index = len(copies)
        copy = pltpu.make_async_remote_copy(
            src_ref=source, dst_ref=target, send_sem=send.at[index], recv_sem=recv.at[index],
            device_id=device, device_id_type=MESH,
        )
        copy.start()
        copies.append(copy)
        return copy

    taken = []

    def arrive(copy):
        if copy is not None and id(copy) not in taken:
            copy.wait_recv()
            taken.append(id(copy))

    pieces = [(row, c, go(*[right_at(ref, row, c) for ref in (right_ref, right_out)], partner)) for c in range(CHUNKS)]
    held = [(row, None)]
    for distance in distances:
        sent = []
        for owner, copy in held:
            arrive(copy)
            source = left_ref if copy is None else left_at(owner)
            sent.append(
                (jnp.bitwise_xor(owner, distance), go(source, left_at(owner), peer_row(distance)))
            )
        held = held + sent
    own = pl.ds(pl.multiple_of(row * rows, rows), rows)
    left_out[:, own, :] = left_ref[...]
    for distance in distances:
        sent = []
        for owner, c, copy in pieces:
            arrive(copy)
            block = right_at(right_out, owner, c)
            sent.append((jnp.bitwise_xor(owner, distance), c, go(block, block, peer_row(distance))))
        pieces = pieces + sent
    for copy in copies:
        copy.wait_send()
        arrive(copy)


def exchange(row_count, sec_count, left, right):
    slots, rows, states = left.shape
    count = row_count - 1 + CHUNKS * row_count
    return pl.pallas_call(
        functools.partial(exchange_kernel, row_count, sec_count // 2),
        out_shape=(
            jax.ShapeDtypeStruct((slots, rows * row_count, states), left.dtype),
            jax.ShapeDtypeStruct(right.shape, right.dtype),
        ),
        in_specs=[VM] * 2,
        out_specs=[VM] * 2,
        scratch_shapes=[pltpu.SemaphoreType.DMA((count,)), pltpu.SemaphoreType.DMA((count,))],
        compiler_params=pltpu.CompilerParams(collective_id=0, has_side_effects=True),
    )(left, right)


def spread(ops, row_of, col_of, same):
    site = ops.shape[0]
    pick_rows = (iota((row_of.shape[0], site), 1) == row_of).astype(BF16)
    pick_cols = (iota((site, col_of.shape[1]), 0) == col_of).astype(BF16)
    out = []
    for part in split2(ops):
        wide = nn(nn(pick_rows, part).astype(BF16), pick_cols)
        out.append(jnp.where(same, wide, 0.0).astype(BF16))
    return out


def inverse_factor(grams, s_ref, t_ref):
    size = grams[0].shape[0]
    slots = len(grams)
    eye = (iota((size, size), 0) == iota((size, size), 1)).astype(F32)
    for s in range(slots):
        s_ref[s] = grams[s]
        t_ref[s] = eye
    sub = iota((PANEL, size), 0)
    lane = iota((PANEL, size), 1)

    def panel(p, carry):
        base = pl.multiple_of(p * PANEL, PANEL)
        for s in range(slots):
            upper = s_ref[s, pl.ds(base, PANEL), :]
            lower = t_ref[s, pl.ds(base, PANEL), :]
            turned = pltpu.roll(upper, lax.rem(size - base, size), 1)
            cols = [jnp.broadcast_to(turned[:, c : c + 1], (PANEL, size)) for c in range(PANEL)]
            for j in range(PANEL):
                scale = lax.rsqrt(cols[j][j : j + 1, :])
                below = jnp.where(sub > j, cols[j] * scale, 0.0)
                at_j = sub == j

                def eliminate(x):
                    pivot = x[j : j + 1, :] * scale
                    return jnp.where(at_j, pivot, x - below * pivot)

                upper, lower = eliminate(upper), eliminate(lower)
                cols = [eliminate(c) if i > j else c for i, c in enumerate(cols)]
            t_ref[s, pl.ds(base, PANEL), :] = lower
            u3, l3 = split3(upper), split3(lower)
            later = lane >= base + PANEL
            m3 = [jnp.where(later, x.astype(F32), 0.0).astype(BF16) for x in u3]
            pairs = ((0, 0), (0, 1), (1, 0), (1, 1), (0, 2), (2, 0))
            lhs = jnp.concatenate([m3[i] for i, _ in pairs], axis=0)
            rhs = jnp.concatenate(
                [jnp.concatenate([u3[k], l3[k]], axis=1) for _, k in pairs], axis=0
            )
            change = tn(lhs, rhs)
            s_ref[s] = s_ref[s] - change[:, :size]
            t_ref[s] = t_ref[s] - change[:, size:]
        return carry

    lax.fori_loop(0, size // PANEL, panel, 0)


def chain_kernel(
    sector_count, left_ref, right_ref, lops_ref, rops_ref, charges_ref, live_ref, kept_ref,
    start_ref, m_out, u_out, part_out, at_ref, b_ref, kl_ref, kr_ref, ga_ref, gah_ref, gal_ref, gbh_ref,
    gbl_ref, s_ref, t_ref,
):
    slots, rows, states = left_ref.shape
    terms, site = lops_ref.shape[0], lops_ref.shape[1]
    cols = right_ref.shape[2]
    width = cols // site
    group = 256 // site
    block = group * site
    sec, row = lax.axis_index("sec"), lax.axis_index("row")
    homes = [sec * slots + s for s in range(slots)]
    mirrors = [lax.rem(h + sector_count // 2, sector_count) for h in homes]
    r0, c0 = iota((block, 1), 0), iota((1, block), 1)
    for t in range(terms):
        parts = spread(lops_ref[t].T, r0 % site, c0 % site, (r0 // site) == (c0 // site))
        for h in range(2):
            kl_ref[h, :, t * block : (t + 1) * block] = parts[h]
        parts = spread(rops_ref[t], r0 // group, c0 // group, (r0 % group) == (c0 % group))
        for h in range(2):
            kr_ref[h, t * block : (t + 1) * block, :] = parts[h]
    for s in range(slots):
        limit = live_ref[homes[s]] * site

        def left_chunk(c, carry):
            base = pl.multiple_of(c * block, block)
            piece = left_ref[s, pl.ds(base, block), :]
            piece = jnp.where(iota((block, states), 0) + base < limit, piece.astype(F32), 0.0)
            turned = piece.T.astype(BF16)
            out = nn(turned, kl_ref[0]) + nn(turned, kl_ref[1])
            for t in range(terms):
                at_ref[s, t * states : (t + 1) * states, pl.ds(base, block)] = out[
                    :, t * block : (t + 1) * block
                ].astype(BF16)
            return carry

        lax.fori_loop(0, rows // block, left_chunk, 0)

        def right_chunk(c, carry):
            base = pl.multiple_of(c * group, group)
            piece = right_ref[s, pl.ds(base, group), :]
            stack = jnp.concatenate([piece[:, j * width : (j + 1) * width] for j in range(site)], axis=0)
            out = (nn(kr_ref[0], stack) + nn(kr_ref[1], stack)).astype(BF16)
            for t in range(terms):
                for i in range(site):
                    b_ref[
                        s, pl.ds(t * states + base, group), i * width : (i + 1) * width
                    ] = out[t * block + i * group : t * block + (i + 1) * group, :]
            return carry

        lax.fori_loop(0, states // group, right_chunk, 0)
        gram = nt(at_ref[s], at_ref[s])
        ga_ref[s] = gram
        gah_ref[s], gal_ref[s] = split2(gram)
        gbh_ref[s], gbl_ref[s] = split2(nt(b_ref[s], b_ref[s]))

    bond = terms * states
    weights = [
        jnp.exp(jnp.full((1, states), charges_ref[m], jnp.int32).astype(F32) * (-chemical))
        for m in mirrors
    ]
    coef = []
    for s in range(slots):
        wanted = start_ref[pl.ds(homes[s], 1), :]
        coef.append((iota((bond, wanted.shape[1]), 0) == wanted).astype(F32))
    for round_index in range(ITERS + 1):
        if round_index < ITERS:
            image = [presplit_nn((gah_ref[s], gal_ref[s]), coef[s]) for s in range(slots)]
        else:
            image = [nn(ga_ref[s], coef[s], HIGHEST) for s in range(slots)]
        inverse_factor([tn(coef[s], image[s], HIGHEST) for s in range(slots)], s_ref, t_ref)
        image = [nt3(image[s], t_ref[s]) for s in range(slots)]
        if round_index < ITERS:
            coef = [
                presplit_nn((gbh_ref[s], gbl_ref[s]), image[s]) * (weights[s] * weights[s])
                for s in range(slots)
            ]
        else:
            coef = [nt3(coef[s], t_ref[s]) for s in range(slots)]
    local_rows = u_out.shape[1]
    total = jnp.zeros((8, states), F32)
    for s in range(slots):
        keep = iota((bond, coef[s].shape[1]), 1) < kept_ref[mirrors[s]]
        out = jnp.where(keep, image[s] * weights[s], 0.0)
        m_out[s] = out.astype(BF16)
        per = out * presplit_nn((gbh_ref[s], gbl_ref[s]), out)
        total = total + jnp.sum(per.reshape(bond // 8, 8, per.shape[1]), axis=0)
        high, low = split2(jnp.where(keep, coef[s], 0.0))
        here = at_ref[s, :, pl.ds(pl.multiple_of(row * local_rows, local_rows), local_rows)]
        u_out[s] = tn(here, high) + tn(here, low)
    part_out[...] = total


def chain(sector_count, left, right, lops, rops, charges, live, kept, start, local_rows):
    slots, rows, states = left.shape
    terms, site = lops.shape[0], lops.shape[1]
    cols, bond, keep = right.shape[2], terms * states, start.shape[1]
    block = 256
    return pl.pallas_call(
        functools.partial(chain_kernel, sector_count),
        out_shape=(
            jax.ShapeDtypeStruct((slots, bond, keep), BF16),
            jax.ShapeDtypeStruct((slots, local_rows, keep), F32),
            jax.ShapeDtypeStruct((8, keep), F32),
        ),
        in_specs=[VM] * 4 + [SM] * 3 + [VM],
        out_specs=[VM] * 3,
        scratch_shapes=[
            pltpu.VMEM((slots, bond, rows), BF16),
            pltpu.VMEM((slots, bond, cols), BF16),
            pltpu.VMEM((2, block, terms * block), BF16),
            pltpu.VMEM((2, terms * block, block), BF16),
            pltpu.VMEM((slots, bond, bond), F32),
            pltpu.VMEM((slots, bond, bond), BF16),
            pltpu.VMEM((slots, bond, bond), BF16),
            pltpu.VMEM((slots, bond, bond), BF16),
            pltpu.VMEM((slots, bond, bond), BF16),
            pltpu.VMEM((slots, keep, keep), F32),
            pltpu.VMEM((slots, keep, keep), F32),
        ],
        compiler_params=pltpu.CompilerParams(vmem_limit_bytes=56 * 2**20),
    )(left, right, lops, rops, charges, live, kept, start)


def deliver_kernel(row_count, sec_count, m_ref, part_ref, m_out, parts_out, m_send, m_recv, send, recv):
    row, sec = lax.axis_index("row"), lax.axis_index("sec")
    depth = m_ref.shape[1] // row_count
    distances = []
    step = row_count // 2
    while step:
        distances.append(step)
        step //= 2
    barrier = pltpu.get_barrier_semaphore()
    for d in range(1, sec_count):
        pl.semaphore_signal(
            barrier, inc=1, device_id=(jnp.bitwise_xor(sec, d), row), device_id_type=MESH
        )
    for d in distances:
        pl.semaphore_signal(
            barrier, inc=1, device_id=(sec, jnp.bitwise_xor(row, d)), device_id_type=MESH
        )
    pl.semaphore_wait(barrier, sec_count - 1 + len(distances))

    def part_of(ref, owner):
        return ref.at[:, pl.ds(pl.multiple_of(owner * depth, depth), depth), :]

    copies, taken = [], []

    def go(source, target, device):
        index = len(copies)
        copy = pltpu.make_async_remote_copy(
            src_ref=source, dst_ref=target, send_sem=m_send.at[index], recv_sem=m_recv.at[index],
            device_id=device, device_id_type=MESH,
        )
        copy.start()
        copies.append(copy)
        return copy

    def arrive(copy):
        if id(copy) not in taken:
            copy.wait_recv()
            taken.append(id(copy))

    partner = (jnp.bitwise_xor(sec, sec_count // 2), row)
    held = [(row, go(part_of(m_ref, row), part_of(m_out, row), partner))]
    small = []
    for d in range(1, sec_count):
        copy = pltpu.make_async_remote_copy(
            src_ref=part_ref, dst_ref=parts_out.at[d], send_sem=send.at[d], recv_sem=recv.at[d],
            device_id=(jnp.bitwise_xor(sec, d), row), device_id_type=MESH,
        )
        copy.start()
        small.append(copy)
    parts_out[0] = part_ref[...]
    for distance in distances:
        sent = []
        for owner, copy in held:
            arrive(copy)
            block = part_of(m_out, owner)
            peer = (sec, jnp.bitwise_xor(row, distance))
            sent.append((jnp.bitwise_xor(owner, distance), go(block, block, peer)))
        held = held + sent
    for copy in small:
        copy.wait()
    for copy in copies:
        copy.wait_send()
        arrive(copy)


def deliver(row_count, sec_count, m, part):
    return pl.pallas_call(
        functools.partial(deliver_kernel, row_count, sec_count),
        out_shape=(
            jax.ShapeDtypeStruct(m.shape, m.dtype),
            jax.ShapeDtypeStruct((sec_count,) + part.shape, part.dtype),
        ),
        in_specs=[VM] * 2,
        out_specs=[VM] * 2,
        scratch_shapes=[
            pltpu.SemaphoreType.DMA((row_count,)),
            pltpu.SemaphoreType.DMA((row_count,)),
            pltpu.SemaphoreType.DMA((sec_count,)),
            pltpu.SemaphoreType.DMA((sec_count,)),
        ],
        compiler_params=pltpu.CompilerParams(collective_id=1, has_side_effects=True),
    )(m, part)


def finish_kernel(row_count, m_ref, parts_ref, right_ref, rops_ref, out_ref, kr_ref, b_ref):
    slots, states, cols = right_ref.shape
    terms, site = rops_ref.shape[0], rops_ref.shape[1]
    width = cols // site
    group = 256 // site
    block = group * site
    here = site // row_count
    part_rows = here * group
    row = lax.axis_index("row")
    r0, c0 = iota((part_rows, 1), 0), iota((1, block), 1)
    for t in range(terms):
        parts = spread(
            rops_ref[t], row * here + r0 // group, c0 // group, (r0 % group) == (c0 % group)
        )
        for h in range(2):
            kr_ref[h, t * part_rows : (t + 1) * part_rows, :] = parts[h]
    total = jnp.sum(jnp.sum(parts_ref[...], axis=0), keepdims=True)
    scale = 1.0 / jnp.sqrt(total)
    for s in range(slots):
        def right_chunk(c, carry):
            base = pl.multiple_of(c * group, group)
            piece = right_ref[s, pl.ds(base, group), :]
            stack = jnp.concatenate([piece[:, j * width : (j + 1) * width] for j in range(site)], axis=0)
            out = (nn(kr_ref[0], stack) + nn(kr_ref[1], stack)).astype(BF16)
            for t in range(terms):
                for i in range(here):
                    b_ref[pl.ds(t * states + base, group), i * width : (i + 1) * width] = out[
                        t * part_rows + i * group : t * part_rows + (i + 1) * group, :
                    ]
            return carry

        lax.fori_loop(0, states // group, right_chunk, 0)
        out_ref[s] = tn(m_ref[s], b_ref[...]) * scale


def finish(row_count, m, parts, right, rops):
    slots, states, cols = right.shape
    terms, site = rops.shape[0], rops.shape[1]
    return pl.pallas_call(
        functools.partial(finish_kernel, row_count),
        out_shape=jax.ShapeDtypeStruct((slots, m.shape[2], cols // row_count), F32),
        in_specs=[VM] * 4,
        out_specs=VM,
        scratch_shapes=[
            pltpu.VMEM((2, terms * 256 // row_count, 256), BF16),
            pltpu.VMEM((terms * states, cols // row_count), BF16),
        ],
        compiler_params=pltpu.CompilerParams(vmem_limit_bytes=40 * 2**20),
    )(m, parts, right, rops)


def solution(mesh):
    row_count, sec_count = mesh.shape["row"], mesh.shape["sec"]

    def on_device(left_block, right_block, left_ops, right_ops, charges, live_states, kept, start):
        left_all, arrived = exchange(row_count, sec_count, left_block, right_block)
        m, basis, part = chain(
            left_block.shape[0] * sec_count, left_all, arrived, left_ops, right_ops,
            charges, live_states, kept, start, left_block.shape[1],
        )
        m, parts = deliver(row_count, sec_count, m, part)
        return basis, finish(row_count, m, parts, right_block, right_ops)

    return jax.shard_map(
        on_device,
        mesh=mesh,
        in_specs=(P("sec", "row", None), P("sec", None, None), P(), P(), P(), P(), P(), P()),
        out_specs=(P("sec", "row", None), P("sec", None, "row")),
        check_vma=False,
    )
```

profile of v0, /device:TPU:0, one launch (start us, length us, event | category | flops | bytes accessed | tf_op | source)
XLA Modules:
  0.0 104.4 jit_solution(12002919440050788281)
XLA Ops:
  0.6 25.7 %shard_map.95 = (bf16[2,2048,128]{2,1,0:T(8,128)(2,1)}, bf16[2,128,2048]{2,1,0:T(8,128)(2,1)}) custom-call(bf16[2,512,128]{2,1,0:T(8,128)(2,1)} %left_ref.1, bf16[2,128,2048]{2,1,0:T(8,128)(2,1)} %right_ref.3), custom_call_target="tpu_custom_call" | custom-call | tf_op jit(solution)/shard_map/pallas_call | solution.py:141
  26.3 0.0 copy-start
  26.3 56.2 %shard_map.96 = (bf16[2,512,128]{2,1,0:T(8,128)(2,1)}, f32[2,512,128]{2,1,0:T(8,128)}, f32[8,128]{1,0:T(8,128)}) custom-call(bf16[2,2048,128]{2,1,0:T(8,128)(2,1)} %get-tuple-element.9.left_ref, bf16[2,128,2048]{2,1,0:T(8,128)(2,1)} %get-tuple-element.10.right_ref, f32[4,16,16]{2,1,0:T(8,128)} %lops_ref.1, f32[4,16,16]{2,1,0:T(8,128)} %rops_ref.3, ...), custom_call_target="tpu_custom_call" | custom-call | tf_op jit(solution)/shard_map/pallas_call | solution.py:309
  82.6 0.0 copy-start.2
  82.6 14.6 %shard_map.97 = (bf16[2,512,128]{2,1,0:T(8,128)(2,1)}, f32[8,8,128]{2,1,0:T(8,128)}) custom-call(bf16[2,512,128]{2,1,0:T(8,128)(2,1)} %get-tuple-element.12.m_ref, f32[8,128]{1,0:T(8,128)} %get-tuple-element.13.part_ref), custom_call_target="tpu_custom_call" | custom-call | tf_op jit(solution)/shard_map/pallas_call | solution.py:401
  97.2 0.0 copy-done
  97.2 0.0 copy-done.2
  97.2 0.0 copy-start.1
  97.3 0.9 copy-done.1
  98.2 0.0 copy-start.3
  98.2 0.8 copy-done.3
  99.0 5.4 %shard_map.98 = f32[2,128,512]{2,1,0:T(8,128)} custom-call(bf16[2,512,128]{2,1,0:T(8,128)(2,1)S(1)} %copy-done.1, f32[8,8,128]{2,1,0:T(8,128)S(1)} %copy-done.3, bf16[2,128,2048]{2,1,0:T(8,128)(2,1)S(1)} %copy-done, f32[4,16,16]{2,1,0:T(8,128)S(1)} %copy-done.2), custom_call_target="tpu_custom_call" | custom-call | tf_op jit(solution)/shard_map/pallas_call | solution.py:457
Async XLA Ops:
  26.3 70.9 %copy-start = (bf16[2,128,2048]{2,1,0:T(8,128)(2,1)S(1)}, bf16[2,128,2048]{2,1,0:T(8,128)(2,1)}, u32[]{:S(2)}) copy-start(bf16[2,128,2048]{2,1,0:T(8,128)(2,1)} %right_ref.3) | copy-start | bytes 3145732
  82.6 14.7 %copy-start.2 = (f32[4,16,16]{2,1,0:T(8,128)S(1)}, f32[4,16,16]{2,1,0:T(8,128)}, u32[]{:S(2)}) copy-start(f32[4,16,16]{2,1,0:T(8,128)} %rops_ref.3) | copy-start | bytes 12292
  97.2 1.0 copy-start.1
  98.2 0.8 copy-start.3
where the time goes:
time: 105 us; the launch traced here: 104 us
  Pallas kernels  102 us (97%)
  local copies, waits for them, and re-layouts  1.71 us (2%)
    pallas_call x1, Pallas kernels, chain(): pl.pallas_call(functools.partial(chain_kernel, sector_count), out_shape=(...  56.2 us
    pallas_call x1, Pallas kernels, exchange(): pl.pallas_call(functools.partial(exchange_kernel, row_count, sec_count //...  25.7 us
    pallas_call x1, Pallas kernels, deliver(): pl.pallas_call(functools.partial(deliver_kernel, row_count, sec_count), o...  14.6 us
    pallas_call x1, Pallas kernels, finish(): pl.pallas_call(functools.partial(finish_kernel, row_count), out_shape=jax...  5.43 us

commit v1 on v0

v1 whole, which is shorter than its diff:
```python
import functools

import jax
import jax.numpy as jnp
from jax import lax
from jax.experimental import pallas as pl
from jax.experimental.pallas import tpu as pltpu
from jax.sharding import PartitionSpec as P

MESH = pl.DeviceIdType.MESH
HIGHEST = lax.Precision.HIGHEST
F32, BF16 = jnp.float32, jnp.bfloat16
chemical = 0.4
ITERS = 2
PANEL = 16
CHUNKS = 2
PIECES = 2
VM = pl.BlockSpec(memory_space=pltpu.VMEM)
SM = pl.BlockSpec(memory_space=pltpu.SMEM)
ANY = pl.BlockSpec(memory_space=pl.ANY)


def nn(a, b, precision=None):
    return lax.dot_general(
        a, b, (((1,), (0,)), ((), ())), precision=precision, preferred_element_type=F32
    )


def nt(a, b, precision=None):
    return lax.dot_general(
        a, b, (((1,), (1,)), ((), ())), precision=precision, preferred_element_type=F32
    )


def tn(a, b, precision=None):
    return lax.dot_general(
        a, b, (((0,), (0,)), ((), ())), precision=precision, preferred_element_type=F32
    )


def split2(x):
    high = x.astype(BF16)
    return high, (x - high.astype(F32)).astype(BF16)


def split3(x):
    high, rest = x.astype(BF16), None
    rest = x - high.astype(F32)
    mid = rest.astype(BF16)
    return high, mid, (rest - mid.astype(F32)).astype(BF16)


def presplit_nn(parts, x):
    high, low = split2(x)
    both = nn(parts[0], jnp.concatenate([high, low], axis=1))
    width = x.shape[1]
    return both[:, :width] + both[:, width:] + nn(parts[1], high)


def nt3(a, b):
    ah, al = split2(a)
    bh, bl = split2(b)
    return nt(jnp.concatenate([ah, al, ah], axis=1), jnp.concatenate([bh, bh, bl], axis=1))


def iota(shape, dim):
    return lax.broadcasted_iota(jnp.int32, shape, dim)


def spread(ops, row_of, col_of, same):
    site = ops.shape[0]
    pick_rows = (iota((row_of.shape[0], site), 1) == row_of).astype(BF16)
    pick_cols = (iota((site, col_of.shape[1]), 0) == col_of).astype(BF16)
    out = []
    for part in split2(ops):
        wide = nn(nn(pick_rows, part).astype(BF16), pick_cols)
        out.append(jnp.where(same, wide, 0.0).astype(BF16))
    return out


def inverse_factor(gram, s_ref, t_ref):
    size = gram.shape[0]
    s_ref[...] = gram
    t_ref[...] = (iota((size, size), 0) == iota((size, size), 1)).astype(F32)
    sub = iota((PANEL, size), 0)
    lane = iota((PANEL, size), 1)

    def panel(p, carry):
        base = pl.multiple_of(p * PANEL, PANEL)
        upper = s_ref[pl.ds(base, PANEL), :]
        lower = t_ref[pl.ds(base, PANEL), :]
        turned = pltpu.roll(upper, lax.rem(size - base, size), 1)
        cols = [jnp.broadcast_to(turned[:, c : c + 1], (PANEL, size)) for c in range(PANEL)]
        for j in range(PANEL):
            scale = lax.rsqrt(cols[j][j : j + 1, :])
            below = jnp.where(sub > j, cols[j] * scale, 0.0)
            at_j = sub == j

            def eliminate(x):
                pivot = x[j : j + 1, :] * scale
                return jnp.where(at_j, pivot, x - below * pivot)

            upper, lower = eliminate(upper), eliminate(lower)
            cols = [eliminate(c) if i > j else c for i, c in enumerate(cols)]
        t_ref[pl.ds(base, PANEL), :] = lower
        u3, l3 = split3(upper), split3(lower)
        later = lane >= base + PANEL
        m3 = [jnp.where(later, x.astype(F32), 0.0).astype(BF16) for x in u3]
        pairs = ((0, 0), (0, 1), (1, 0), (1, 1), (0, 2), (2, 0))
        lhs = jnp.concatenate([m3[i] for i, _ in pairs], axis=0)
        rhs = jnp.concatenate([jnp.concatenate([u3[k], l3[k]], axis=1) for _, k in pairs], axis=0)
        change = tn(lhs, rhs)
        s_ref[...] = s_ref[...] - change[:, :size]
        t_ref[...] = t_ref[...] - change[:, size:]
        return carry

    lax.fori_loop(0, size // PANEL, panel, 0)


def halvings(count):
    out, step = [], count // 2
    while step:
        out.append(step)
        step //= 2
    return out


def gate_kernel(
    row_count, sec_count, left_hbm, right_hbm, lops_ref, rops_ref, charges_ref, live_ref, kept_ref,
    start_ref, u_out, w_out, lown, lrecv, rown, rpart, kl_ref, kr_ref, at_ref, own_ref, b_ref, bw_ref,
    ga_ref, gah_ref, gal_ref, gbh_ref, gbl_ref, s_ref, t_ref, csend, crecv, msend, mrecv, total_ref,
    local, lsend, lget, fsend, fget, csems, cgets, msems, mgets, tsems, tgets,
):
    slots, rows, states = left_hbm.shape
    terms, site = lops_ref.shape[0], lops_ref.shape[1]
    cols = right_hbm.shape[2]
    width = cols // site
    group = 256 // site
    block = group * site
    bond = terms * states
    keep = start_ref.shape[1]
    sector_count = slots * sec_count
    mates = row_count // slots
    here = site // row_count
    piece = rows // PIECES
    half = sec_count // 2

    sec, row = lax.axis_index("sec"), lax.axis_index("row")
    slot, mate = row // mates, row % mates
    partner = jnp.bitwise_xor(sec, half)
    home = sec * slots + slot
    mirror = lax.rem(home + sector_count // 2, sector_count)

    def slot_row(t):
        return t * mates + mate

    def other_slot(d):
        return lax.rem(slot + d, slots)

    def other_mate(d):
        return lax.rem(mate + d, mates)

    neighbours = [d for d in halvings(sec_count) if d != half]
    greeted = [(partner, slot_row(t)) for t in range(slots)]
    greeted += [(sec, slot_row(other_slot(d))) for d in range(1, slots)]
    greeted += [(sec, slot * mates + other_mate(d)) for d in range(1, mates)]
    greeted += [(jnp.bitwise_xor(sec, d), row) for d in neighbours]
    barrier = pltpu.get_barrier_semaphore()
    for device in greeted:
        pl.semaphore_signal(barrier, inc=1, device_id=device, device_id_type=MESH)

    near = [pltpu.make_async_copy(right_hbm.at[slot], rown, local.at[0])]
    near.append(pltpu.make_async_copy(left_hbm, lown, local.at[1]))
    for copy in near:
        copy.start()

    r0, c0 = iota((block, 1), 0), iota((1, block), 1)
    for t in range(terms):
        parts = spread(rops_ref[t], r0 // group, c0 // group, (r0 % group) == (c0 % group))
        for h in range(2):
            kr_ref[h, t * block : (t + 1) * block, :] = parts[h]

    pl.semaphore_wait(barrier, len(greeted))

    def remote(source, target, send, recv, device):
        return pltpu.make_async_remote_copy(
            src_ref=source, dst_ref=target, send_sem=send, recv_sem=recv,
            device_id=device, device_id_type=MESH,
        )

    def rows_at(owner, k):
        return pl.ds(pl.multiple_of(owner * rows + k * piece, piece), piece)

    sent = []
    for k in range(PIECES):
        for t in range(slots):
            copy = remote(
                left_hbm.at[t, pl.ds(k * piece, piece), :], lrecv.at[rows_at(row, k), :],
                lsend.at[t, k], lget.at[slot, k], (partner, slot_row(t)),
            )
            copy.start()
            sent.append(copy)

    for t in range(terms):
        parts = spread(lops_ref[t].T, r0 % site, c0 % site, (r0 // site) == (c0 // site))
        for h in range(2):
            kl_ref[h, :, t * block : (t + 1) * block] = parts[h]
    for copy in near:
        copy.wait()

    def right_chunk(c, carry):
        base = pl.multiple_of(c * group, group)
        part = rown[pl.ds(base, group), :]
        stack = jnp.concatenate([part[:, j * width : (j + 1) * width] for j in range(site)], axis=0)
        out = (nn(kr_ref[0], stack) + nn(kr_ref[1], stack)).astype(BF16)
        for t in range(terms):
            for i in range(site):
                b_ref[pl.ds(t * states + base, group), i * width : (i + 1) * width] = out[
                    t * block + i * group : t * block + (i + 1) * group, :
                ]
        return carry

    lax.fori_loop(0, states // group, right_chunk, 0)
    gbh_ref[...], gbl_ref[...] = split2(nt(b_ref[...], b_ref[...]))

    def gate_left(part, first, limit, store):
        part = jnp.where(iota((block, states), 0) + first < limit, part.astype(F32), 0.0)
        turned = part.T.astype(BF16)
        out = nn(turned, kl_ref[0]) + nn(turned, kl_ref[1])
        for t in range(terms):
            store(t, out[:, t * block : (t + 1) * block].astype(BF16))

    limit = live_ref[mirror] * site
    forwarded = []
    for k in range(PIECES):
        arrived = []
        for t in range(slots):
            owner = slot_row(t)
            place = lrecv.at[rows_at(owner, k), :]
            remote(place, place, lsend.at[t, k], lget.at[t, k], (partner, owner)).wait_recv()
            for d in range(1, mates):
                copy = remote(
                    place, place, fsend.at[d - 1, t, k], fget.at[d - 1, t, k],
                    (sec, slot * mates + other_mate(d)),
                )
                copy.start()
                forwarded.append(copy)
            arrived.append((owner, None))
        for d in range(1, mates):
            for t in range(slots):
                owner = t * mates + other_mate(mates - d)
                place = lrecv.at[rows_at(owner, k), :]
                arrived.append((owner, remote(
                    place, place, fsend.at[d - 1, t, k], fget.at[d - 1, t, k],
                    (sec, slot * mates + other_mate(mates - d)),
                )))
        for index, (owner, copy) in enumerate(arrived):
            if copy is not None:
                copy.wait_recv()
            for q in range(piece // block):
                column = ((k * row_count + index) * (piece // block) + q) * block

                def store(t, value):
                    at_ref[t * states : (t + 1) * states, column : column + block] = value

                first = owner * rows + k * piece + q * block
                gate_left(lrecv[pl.ds(pl.multiple_of(first, block), block), :], first, limit, store)
        span = row_count * piece
        gram = nt(at_ref[:, k * span : (k + 1) * span], at_ref[:, k * span : (k + 1) * span])
        ga_ref[...] = gram if k == 0 else ga_ref[...] + gram
    gah_ref[...], gal_ref[...] = split2(ga_ref[...])
    for copy in sent + forwarded:
        copy.wait_send()

    weight = jnp.exp(jnp.full((1, states), charges_ref[home], jnp.int32).astype(F32) * (-chemical))
    coef = (iota((bond, keep), 0) == start_ref[pl.ds(mirror, 1), :]).astype(F32)
    for round_index in range(ITERS + 1):
        if round_index < ITERS:
            image = presplit_nn((gah_ref[...], gal_ref[...]), coef)
        else:
            image = nn(ga_ref[...], coef, HIGHEST)
        inverse_factor(tn(coef, image, HIGHEST), s_ref, t_ref)
        image = nt3(image, t_ref[...])
        if round_index < ITERS:
            coef = presplit_nn((gbh_ref[...], gbl_ref[...]), image) * (weight * weight)
        else:
            coef = nt3(coef, t_ref[...])
    kept_here = iota((bond, keep), 1) < kept_ref[home]
    csend[...] = jnp.where(kept_here, coef, 0.0).astype(BF16)
    out = jnp.where(kept_here, image * weight, 0.0)
    msend[...] = out.astype(BF16)
    per = out * presplit_nn((gbh_ref[...], gbl_ref[...]), out)
    total_ref[0] = jnp.sum(per.reshape(bond // 8, 8, keep), axis=0)

    part = bond // mates

    def coef_at(t, m):
        return crecv.at[t, pl.ds(pl.multiple_of(m * part, part), part), :]

    flying = []

    def go(*args):
        copy = remote(*args)
        copy.start()
        flying.append(copy)

    go(
        csend.at[pl.ds(pl.multiple_of(mate * part, part), part), :], coef_at(slot, mate),
        csems.at[0], cgets.at[0], (partner, row),
    )
    for d in range(1, slots):
        go(msend, mrecv.at[slot], msems.at[d - 1], mgets.at[d - 1], (sec, slot_row(other_slot(d))))
    for d in range(1, slots):
        go(total_ref.at[0], total_ref.at[d], tsems.at[d - 1], tgets.at[d - 1], (sec, slot_row(other_slot(d))))

    def own_chunk(c, carry):
        t = c // (rows // block)
        q = lax.rem(c, rows // block)
        first = pl.multiple_of(q * block, block)

        def store(term, value):
            own_ref[t, term * states : (term + 1) * states, pl.ds(first, block)] = value

        owner = lax.rem(sec * slots + t, sector_count)
        gate_left(
            lown[t, pl.ds(first, block), :], row * rows + first, live_ref[owner] * site, store
        )
        return carry

    lax.fori_loop(0, slots * (rows // block), own_chunk, 0)

    part_rows = here * group
    part_cols = cols // row_count
    for d in range(slots):
        t = other_slot(d)
        if d == 0:
            bw_ref[t] = b_ref[:, pl.ds(pl.multiple_of(row * part_cols, part_cols), part_cols)]
            continue
        again = pltpu.make_async_copy(right_hbm.at[t], rown, local.at[0])
        again.start()
        again.wait()

        def part_chunk(c, carry):
            base = pl.multiple_of(c * group, group)
            piece_rows = rown[pl.ds(base, group), :]
            stack = jnp.concatenate(
                [piece_rows[:, j * width : (j + 1) * width] for j in range(site)], axis=0
            )
            pick = [
                jnp.concatenate([
                    kr_ref[h, pl.ds(pl.multiple_of(term * block + row * part_rows, part_rows), part_rows), :]
                    for term in range(terms)
                ], axis=0)
                for h in range(2)
            ]
            out = (nn(pick[0], stack) + nn(pick[1], stack)).astype(BF16)
            for term in range(terms):
                for i in range(here):
                    bw_ref[t, pl.ds(term * states + base, group), i * width : (i + 1) * width] = out[
                        term * part_rows + i * group : term * part_rows + (i + 1) * group, :
                    ]
            return carry

        lax.fori_loop(0, states // group, part_chunk, 0)

    summed = total_ref[0]
    for d in range(1, slots):
        flying_at = remote(
            total_ref.at[0], total_ref.at[d], tsems.at[d - 1], tgets.at[d - 1], (sec, slot_row(other_slot(d)))
        )
        flying_at.wait_recv()
        summed = summed + total_ref[d]
    index = slots
    for number, d in enumerate(halvings(sec_count)):
        total_ref[index] = summed
        copy = remote(
            total_ref.at[index], total_ref.at[index + 1], tsems.at[slots - 1 + number],
            tgets.at[slots - 1 + number], (jnp.bitwise_xor(sec, d), row),
        )
        copy.start()
        copy.wait()
        summed = summed + total_ref[index + 1]
        index += 2
    scale = 1.0 / jnp.sqrt(jnp.sum(summed, keepdims=True))

    flying[0].wait_recv()
    for d in range(1, slots):
        go(
            coef_at(slot, mate), coef_at(slot, mate), csems.at[d], cgets.at[d],
            (sec, slot_row(other_slot(d))),
        )
    number = slots
    for d in range(1, mates):
        go(
            coef_at(slot, mate), coef_at(slot, mate), csems.at[number], cgets.at[number],
            (sec, slot * mates + other_mate(d)),
        )
        number += 1
    for e in range(1, slots):
        t = other_slot(slots - e)
        remote(
            coef_at(t, mate), coef_at(t, mate), csems.at[e], cgets.at[e], (sec, slot_row(t))
        ).wait_recv()
        for d in range(1, mates):
            go(
                coef_at(t, mate), coef_at(t, mate), csems.at[number], cgets.at[number],
                (sec, slot * mates + other_mate(d)),
            )
            number += 1

    for d in range(1, slots):
        t = other_slot(slots - d)
        remote(
            msend, mrecv.at[t], msems.at[d - 1], mgets.at[d - 1], (sec, slot_row(t))
        ).wait_recv()
        w_out[t] = tn(mrecv[t], bw_ref[t]) * scale
    w_out[slot] = tn(msend[...], bw_ref[slot]) * scale

    number = slots
    for d in range(1, mates):
        remote(
            coef_at(slot, mate), coef_at(slot, other_mate(mates - d)), csems.at[number],
            cgets.at[number], (sec, slot * mates + other_mate(mates - d)),
        ).wait_recv()
        number += 1
    for e in range(1, slots):
        t = other_slot(slots - e)
        for d in range(1, mates):
            remote(
                coef_at(t, mate), coef_at(t, other_mate(mates - d)), csems.at[number],
                cgets.at[number], (sec, slot * mates + other_mate(mates - d)),
            ).wait_recv()
            number += 1
    for t in range(slots):
        u_out[t] = tn(own_ref[t], crecv[t])
    for copy in flying:
        copy.wait_send()


def solution(mesh):
    row_count, sec_count = mesh.shape["row"], mesh.shape["sec"]

    def on_device(left_block, right_block, left_ops, right_ops, charges, live_states, kept, start):
        slots, rows, states = left_block.shape
        terms, site = left_ops.shape[0], left_ops.shape[1]
        cols, bond, keep = right_block.shape[2], terms * states, start.shape[1]
        block, mates = 256, row_count // slots
        part_cols = cols // row_count
        steps = len(halvings(sec_count))
        coef_copies = slots + slots * (mates - 1)
        dma = pltpu.SemaphoreType.DMA
        return pl.pallas_call(
            functools.partial(gate_kernel, row_count, sec_count),
            out_shape=(
                jax.ShapeDtypeStruct((slots, rows, keep), F32),
                jax.ShapeDtypeStruct((slots, keep, part_cols), F32),
            ),
            in_specs=[ANY] * 2 + [VM] * 2 + [SM] * 3 + [VM],
            out_specs=[VM] * 2,
            scratch_shapes=[
                pltpu.VMEM((slots, rows, states), BF16),
                pltpu.VMEM((rows * row_count, states), BF16),
                pltpu.VMEM((states, cols), BF16),
                pltpu.VMEM((8, 128), BF16),
                pltpu.VMEM((2, block, terms * block), BF16),
                pltpu.VMEM((2, terms * block, block), BF16),
                pltpu.VMEM((bond, rows * row_count), BF16),
                pltpu.VMEM((slots, bond, rows), BF16),
                pltpu.VMEM((bond, cols), BF16),
                pltpu.VMEM((slots, bond, part_cols), BF16),
                pltpu.VMEM((bond, bond), F32),
                pltpu.VMEM((bond, bond), BF16),
                pltpu.VMEM((bond, bond), BF16),
                pltpu.VMEM((bond, bond), BF16),
                pltpu.VMEM((bond, bond), BF16),
                pltpu.VMEM((keep, keep), F32),
                pltpu.VMEM((keep, keep), F32),
                pltpu.VMEM((bond, keep), BF16),
                pltpu.VMEM((slots, bond, keep), BF16),
                pltpu.VMEM((bond, keep), BF16),
                pltpu.VMEM((slots, bond, keep), BF16),
                pltpu.VMEM((slots + 2 * steps, 8, keep), F32),
                dma((2,)),
                dma((slots, PIECES)), dma((slots, PIECES)),
                dma((mates - 1, slots, PIECES)), dma((mates - 1, slots, PIECES)),
                dma((coef_copies,)), dma((coef_copies,)),
                dma((slots - 1,)), dma((slots - 1,)),
                dma((slots - 1 + steps,)), dma((slots - 1 + steps,)),
            ],
            compiler_params=pltpu.CompilerParams(
                collective_id=0, has_side_effects=True, vmem_limit_bytes=56 * 2**20
            ),
        )(left_block, right_block, left_ops, right_ops, charges, live_states, kept, start)

    return jax.shard_map(
        on_device,
        mesh=mesh,
        in_specs=(P("sec", "row", None), P("sec", None, None), P(), P(), P(), P(), P(), P()),
        out_specs=(P("sec", "row", None), P("sec", None, "row")),
        check_vma=False,
    )
```

time: 105 us -> 63.4 us (0.60)
  Pallas kernels: 102 us -> 59.4 us
    pallas_call x4 -> x1, Pallas kernels: 102 us -> 59.4 us  [on_device(): pl.pallas_call(functools.partial(gate_kernel, row_count, sec_count), out_...]
    unnamed x8 -> x4, local copies, waits for them, and re-layouts: 1.71 us -> 2.72 us
where the time goes in v1:
time: 63.4 us; the launch traced here: 62.7 us
  Pallas kernels  59.4 us (94%)
  local copies, waits for them, and re-layouts  2.72 us (4%)
  between operations  0.65 us (1%)
    pallas_call x1, Pallas kernels, on_device(): pl.pallas_call(functools.partial(gate_kernel, row_count, sec_count), out_...  59.4 us
    unnamed x4, local copies, waits for them, and re-layouts  2.72 us

profile of v1, /device:TPU:0, one launch (start us, length us, event | category | flops | bytes accessed | tf_op | source)
XLA Modules:
  0.0 62.7 jit_solution(16741464262275613497)
XLA Ops:
  0.6 59.4 %shard_map.95 = (f32[2,512,128]{2,1,0:T(8,128)}, f32[2,128,512]{2,1,0:T(8,128)}) custom-call(bf16[2,512,128]{2,1,0:T(8,128)(2,1)} %left_hbm.1, bf16[2,128,2048]{2,1,0:T(8,128)(2,1)} %right_hbm.1, f32[4,16,16]{2,1,0:T(8,128)} %lops_ref.1, f32[4,16,16]{2,1,0:T(8,128)} %rops_ref.1, s32[16]{0:T(128)} %charges_ref.1, s32[16]{0:T(128)} %live_ref.1, s32[16]{0:T(128)} %kept_ref.1, ...), custom_call_target="tpu_custom_call" | custom-call | tf_op jit(solution)/shard_map/pallas_call | solution.py:452
  60.0 0.0 copy-start
  60.0 1.9 %copy.12 = f32[2,512,128]{2,1,0:T(8,128)} copy(f32[2,512,128]{2,1,0:T(8,128)} %get-tuple-element.4) | data formatting | bytes 1048576
  61.9 0.0 copy-done
  61.9 0.8 %copy.13 = f32[2,128,512]{2,1,0:T(8,128)} copy(f32[2,128,512]{2,1,0:T(8,128)S(1)} %copy-done) | data formatting | bytes 1048576
Async XLA Ops:
  60.0 1.9 %copy-start = (f32[2,128,512]{2,1,0:T(8,128)S(1)}, f32[2,128,512]{2,1,0:T(8,128)}, u32[]{:S(2)}) copy-start(f32[2,128,512]{2,1,0:T(8,128)} %get-tuple-element.5) | copy-start | bytes 1572868

commit v2 on v1

--- a/solution.py
+++ b/solution.py
@@ -117,18 +117,11 @@
     lax.fori_loop(0, size // PANEL, panel, 0)
 
 
-def halvings(count):
-    out, step = [], count // 2
-    while step:
-        out.append(step)
-        step //= 2
-    return out
-
-
 def gate_kernel(
-    row_count, sec_count, left_hbm, right_hbm, lops_ref, rops_ref, charges_ref, live_ref, kept_ref,
-    start_ref, u_out, w_out, lown, lrecv, rown, rpart, kl_ref, kr_ref, at_ref, own_ref, b_ref, bw_ref,
-    ga_ref, gah_ref, gal_ref, gbh_ref, gbl_ref, s_ref, t_ref, csend, crecv, msend, mrecv, total_ref,
+    row_count, sec_count, left_hbm, right_hbm, lops_hbm, rops_hbm, charges_hbm, live_hbm, kept_hbm,
+    start_hbm, u_hbm, w_hbm, lops_ref, rops_ref, charges_ref, live_ref, kept_ref, start_ref, u_out, w_out,
+    lown, lrecv, rown, kl_ref, kr_ref, at_ref, own_ref, b_ref, bw_ref, ga_ref, gah_ref, gal_ref,
+    gbh_ref, gbl_ref, s_ref, t_ref, csend, crecv, msend, mrecv, total_ref,
     local, lsend, lget, fsend, fget, csems, cgets, msems, mgets, tsems, tgets,
 ):
     slots, rows, states = left_hbm.shape
@@ -160,19 +153,29 @@
     def other_mate(d):
         return lax.rem(mate + d, mates)
 
-    neighbours = [d for d in halvings(sec_count) if d != half]
-    greeted = [(partner, slot_row(t)) for t in range(slots)]
-    greeted += [(sec, slot_row(other_slot(d))) for d in range(1, slots)]
-    greeted += [(sec, slot * mates + other_mate(d)) for d in range(1, mates)]
-    greeted += [(jnp.bitwise_xor(sec, d), row) for d in neighbours]
+    greeted = [(sec, slot * mates + other_mate(d)) for d in range(1, mates)]
+    greeted += [
+        (jnp.bitwise_xor(sec, d), slot_row(other_slot(e)))
+        for d in range(sec_count) for e in range(slots) if d or e
+    ]
     barrier = pltpu.get_barrier_semaphore()
     for device in greeted:
         pl.semaphore_signal(barrier, inc=1, device_id=device, device_id_type=MESH)
 
-    near = [pltpu.make_async_copy(right_hbm.at[slot], rown, local.at[0])]
-    near.append(pltpu.make_async_copy(left_hbm, lown, local.at[1]))
+    near = [
+        pltpu.make_async_copy(source, target, local.at[i])
+        for i, (source, target) in enumerate((
+            (rops_hbm, rops_ref), (lops_hbm, lops_ref), (charges_hbm, charges_ref), (live_hbm, live_ref),
+            (kept_hbm, kept_ref), (start_hbm, start_ref), (left_hbm, lown),
+        ))
+    ]
+    near += [
+        pltpu.make_async_copy(right_hbm.at[other_slot(e)], rown.at[e], local.at[len(near) + e])
+        for e in range(slots)
+    ]
     for copy in near:
         copy.start()
+    near[0].wait()
 
     r0, c0 = iota((block, 1), 0), iota((1, block), 1)
     for t in range(terms):
@@ -201,16 +204,16 @@
             copy.start()
             sent.append(copy)
 
+    for copy in near[1:]:
+        copy.wait()
     for t in range(terms):
         parts = spread(lops_ref[t].T, r0 % site, c0 % site, (r0 // site) == (c0 // site))
         for h in range(2):
             kl_ref[h, :, t * block : (t + 1) * block] = parts[h]
-    for copy in near:
-        copy.wait()
 
     def right_chunk(c, carry):
         base = pl.multiple_of(c * group, group)
-        part = rown[pl.ds(base, group), :]
+        part = rown[0, pl.ds(base, group), :]
         stack = jnp.concatenate([part[:, j * width : (j + 1) * width] for j in range(site)], axis=0)
         out = (nn(kr_ref[0], stack) + nn(kr_ref[1], stack)).astype(BF16)
         for t in range(terms):
@@ -280,22 +283,22 @@
         else:
             image = nn(ga_ref[...], coef, HIGHEST)
         inverse_factor(tn(coef, image, HIGHEST), s_ref, t_ref)
-        image = nt3(image, t_ref[...])
         if round_index < ITERS:
+            image = nt3(image, t_ref[...])
             coef = presplit_nn((gbh_ref[...], gbl_ref[...]), image) * (weight * weight)
-        else:
-            coef = nt3(coef, t_ref[...])
     kept_here = iota((bond, keep), 1) < kept_ref[home]
-    csend[...] = jnp.where(kept_here, coef, 0.0).astype(BF16)
-    out = jnp.where(kept_here, image * weight, 0.0)
+    csend[...] = jnp.where(kept_here, nt3(coef, t_ref[...]), 0.0).astype(BF16)
+    out = jnp.where(kept_here, nt3(image, t_ref[...]) * weight, 0.0)
     msend[...] = out.astype(BF16)
-    per = out * presplit_nn((gbh_ref[...], gbl_ref[...]), out)
-    total_ref[0] = jnp.sum(per.reshape(bond // 8, 8, keep), axis=0)
 
     part = bond // mates
-
-    def coef_at(t, m):
-        return crecv.at[t, pl.ds(pl.multiple_of(m * part, part), part), :]
+    bit = part // PIECES
+
+    def coef_rows(m, k):
+        return pl.ds(pl.multiple_of(m * part + k * bit, bit), bit)
+
+    def coef_at(t, m, k):
+        return crecv.at[t, coef_rows(m, k), :]
 
     flying = []
 
@@ -304,14 +307,23 @@
         copy.start()
         flying.append(copy)
 
-    go(
-        csend.at[pl.ds(pl.multiple_of(mate * part, part), part), :], coef_at(slot, mate),
-        csems.at[0], cgets.at[0], (partner, row),
-    )
+    for k in range(PIECES):
+        go(
+            csend.at[coef_rows(mate, k), :], coef_at(slot, mate, k), csems.at[0, k], cgets.at[0, k],
+            (partner, row),
+        )
+    per = out * presplit_nn((gbh_ref[...], gbl_ref[...]), out)
     for d in range(1, slots):
         go(msend, mrecv.at[slot], msems.at[d - 1], mgets.at[d - 1], (sec, slot_row(other_slot(d))))
-    for d in range(1, slots):
-        go(total_ref.at[0], total_ref.at[d], tsems.at[d - 1], tgets.at[d - 1], (sec, slot_row(other_slot(d))))
+    total_ref[0] = jnp.sum(per, axis=0, keepdims=True)
+    for d in range(sec_count):
+        for e in range(slots):
+            if d or e:
+                index = d * slots + e
+                go(
+                    total_ref.at[0], total_ref.at[index], tsems.at[index], tgets.at[index],
+                    (jnp.bitwise_xor(sec, d), slot_row(other_slot(e))),
+                )
 
     def own_chunk(c, carry):
         t = c // (rows // block)
@@ -321,7 +333,7 @@
         def store(term, value):
             own_ref[t, term * states : (term + 1) * states, pl.ds(first, block)] = value
 
-        owner = lax.rem(sec * slots + t, sector_count)
+        owner = sec * slots + t
         gate_left(
             lown[t, pl.ds(first, block), :], row * rows + first, live_ref[owner] * site, store
         )
@@ -331,110 +343,99 @@
 
     part_rows = here * group
     part_cols = cols // row_count
-    for d in range(slots):
-        t = other_slot(d)
-        if d == 0:
-            bw_ref[t] = b_ref[:, pl.ds(pl.multiple_of(row * part_cols, part_cols), part_cols)]
-            continue
-        again = pltpu.make_async_copy(right_hbm.at[t], rown, local.at[0])
-        again.start()
-        again.wait()
-
-        def part_chunk(c, carry):
-            base = pl.multiple_of(c * group, group)
-            piece_rows = rown[pl.ds(base, group), :]
-            stack = jnp.concatenate(
-                [piece_rows[:, j * width : (j + 1) * width] for j in range(site)], axis=0
-            )
-            pick = [
-                jnp.concatenate([
-                    kr_ref[h, pl.ds(pl.multiple_of(term * block + row * part_rows, part_rows), part_rows), :]
-                    for term in range(terms)
-                ], axis=0)
-                for h in range(2)
-            ]
-            out = (nn(pick[0], stack) + nn(pick[1], stack)).astype(BF16)
-            for term in range(terms):
-                for i in range(here):
-                    bw_ref[t, pl.ds(term * states + base, group), i * width : (i + 1) * width] = out[
-                        term * part_rows + i * group : term * part_rows + (i + 1) * group, :
-                    ]
-            return carry
-
-        lax.fori_loop(0, states // group, part_chunk, 0)
-
-    summed = total_ref[0]
-    for d in range(1, slots):
-        flying_at = remote(
-            total_ref.at[0], total_ref.at[d], tsems.at[d - 1], tgets.at[d - 1], (sec, slot_row(other_slot(d)))
-        )
-        flying_at.wait_recv()
-        summed = summed + total_ref[d]
-    index = slots
-    for number, d in enumerate(halvings(sec_count)):
-        total_ref[index] = summed
-        copy = remote(
-            total_ref.at[index], total_ref.at[index + 1], tsems.at[slots - 1 + number],
-            tgets.at[slots - 1 + number], (jnp.bitwise_xor(sec, d), row),
-        )
-        copy.start()
-        copy.wait()
-        summed = summed + total_ref[index + 1]
-        index += 2
-    scale = 1.0 / jnp.sqrt(jnp.sum(summed, keepdims=True))
-
-    flying[0].wait_recv()
-    for d in range(1, slots):
-        go(
-            coef_at(slot, mate), coef_at(slot, mate), csems.at[d], cgets.at[d],
-            (sec, slot_row(other_slot(d))),
-        )
-    number = slots
-    for d in range(1, mates):
-        go(
-            coef_at(slot, mate), coef_at(slot, mate), csems.at[number], cgets.at[number],
-            (sec, slot * mates + other_mate(d)),
-        )
-        number += 1
-    for e in range(1, slots):
-        t = other_slot(slots - e)
-        remote(
-            coef_at(t, mate), coef_at(t, mate), csems.at[e], cgets.at[e], (sec, slot_row(t))
-        ).wait_recv()
+    bw_ref[0] = b_ref[:, pl.ds(pl.multiple_of(row * part_cols, part_cols), part_cols)]
+
+    def part_chunk(c, carry):
+        e = 1 + c // (states // group)
+        base = pl.multiple_of(lax.rem(c, states // group) * group, group)
+        piece_rows = rown[e, pl.ds(base, group), :]
+        stack = jnp.concatenate([piece_rows[:, j * width : (j + 1) * width] for j in range(site)], axis=0)
+        pick = [
+            jnp.concatenate([
+                kr_ref[h, pl.ds(pl.multiple_of(term * block + row * part_rows, part_rows), part_rows), :]
+                for term in range(terms)
+            ], axis=0)
+            for h in range(2)
+        ]
+        out = (nn(pick[0], stack) + nn(pick[1], stack)).astype(BF16)
+        for term in range(terms):
+            for i in range(here):
+                bw_ref[e, pl.ds(term * states + base, group), i * width : (i + 1) * width] = out[
+                    term * part_rows + i * group : term * part_rows + (i + 1) * group, :
+                ]
+        return carry
+
+    lax.fori_loop(0, (slots - 1) * (states // group), part_chunk, 0)
+
+    def pass_on(t, m, k, index):
         for d in range(1, mates):
             go(
-                coef_at(t, mate), coef_at(t, mate), csems.at[number], cgets.at[number],
+                coef_at(t, m, k), coef_at(t, m, k), csems.at[index + d - 1, k], cgets.at[index + d - 1, k],
                 (sec, slot * mates + other_mate(d)),
             )
-            number += 1
-
+
+    for k in range(PIECES):
+        flying[k].wait_recv()
+        for e in range(1, slots):
+            go(
+                coef_at(slot, mate, k), coef_at(slot, mate, k), csems.at[e, k], cgets.at[e, k],
+                (sec, slot_row(other_slot(e))),
+            )
+        pass_on(slot, mate, k, slots)
+    for k in range(PIECES):
+        for e in range(1, slots):
+            t = other_slot(slots - e)
+            remote(
+                coef_at(t, mate, k), coef_at(t, mate, k), csems.at[e, k], cgets.at[e, k], (sec, slot_row(t))
+            ).wait_recv()
+            pass_on(t, mate, k, slots + e * (mates - 1))
+
+    wide = [tn(msend[...], bw_ref[0])]
     for d in range(1, slots):
         t = other_slot(slots - d)
         remote(
             msend, mrecv.at[t], msems.at[d - 1], mgets.at[d - 1], (sec, slot_row(t))
         ).wait_recv()
-        w_out[t] = tn(mrecv[t], bw_ref[t]) * scale
-    w_out[slot] = tn(msend[...], bw_ref[slot]) * scale
-
-    number = slots
-    for d in range(1, mates):
-        remote(
-            coef_at(slot, mate), coef_at(slot, other_mate(mates - d)), csems.at[number],
-            cgets.at[number], (sec, slot * mates + other_mate(mates - d)),
-        ).wait_recv()
-        number += 1
-    for e in range(1, slots):
+        wide.append(tn(mrecv[t], bw_ref[slots - d]))
+    summed = total_ref[0]
+    for d in range(sec_count):
+        for e in range(slots):
+            if d or e:
+                index = d * slots + e
+                remote(
+                    total_ref.at[0], total_ref.at[index], tsems.at[index], tgets.at[index],
+                    (jnp.bitwise_xor(sec, d), slot_row(other_slot(slots - e))),
+                ).wait_recv()
+                summed = summed + total_ref[index]
+    scale = 1.0 / jnp.sqrt(jnp.sum(summed, keepdims=True))
+    leaving = []
+
+    def leave(source, target):
+        copy = pltpu.make_async_copy(source, target, local.at[len(leaving)])
+        copy.start()
+        leaving.append(copy)
+
+    for d in range(slots):
+        t = other_slot(slots - d)
+        w_out[d] = wide[d] * scale
+        leave(w_out.at[d], w_hbm.at[t])
+
+    for e in range(slots):
         t = other_slot(slots - e)
-        for d in range(1, mates):
-            remote(
-                coef_at(t, mate), coef_at(t, other_mate(mates - d)), csems.at[number],
-                cgets.at[number], (sec, slot * mates + other_mate(mates - d)),
-            ).wait_recv()
-            number += 1
-    for t in range(slots):
-        u_out[t] = tn(own_ref[t], crecv[t])
+        for k in range(PIECES):
+            for d in range(1, mates):
+                index = slots + e * (mates - 1) + d - 1
+                m = other_mate(mates - d)
+                remote(
+                    coef_at(t, m, k), coef_at(t, m, k), csems.at[index, k], cgets.at[index, k],
+                    (sec, slot * mates + m),
+                ).wait_recv()
+        u_out[e] = tn(own_ref[t], crecv[t])
+        leave(u_out.at[e], u_hbm.at[t])
     for copy in flying:
         copy.wait_send()
+    for copy in leaving:
+        copy.wait()
 
 
 def solution(mesh):
@@ -446,8 +447,8 @@
         cols, bond, keep = right_block.shape[2], terms * states, start.shape[1]
         block, mates = 256, row_count // slots
         part_cols = cols // row_count
-        steps = len(halvings(sec_count))
         coef_copies = slots + slots * (mates - 1)
+        peers = slots * sec_count
         dma = pltpu.SemaphoreType.DMA
         return pl.pallas_call(
             functools.partial(gate_kernel, row_count, sec_count),
@@ -455,13 +456,20 @@
                 jax.ShapeDtypeStruct((slots, rows, keep), F32),
                 jax.ShapeDtypeStruct((slots, keep, part_cols), F32),
             ),
-            in_specs=[ANY] * 2 + [VM] * 2 + [SM] * 3 + [VM],
-            out_specs=[VM] * 2,
+            in_specs=[ANY] * 8,
+            out_specs=[ANY] * 2,
             scratch_shapes=[
+                pltpu.VMEM(left_ops.shape, F32),
+                pltpu.VMEM(right_ops.shape, F32),
+                pltpu.SMEM(charges.shape, jnp.int32),
+                pltpu.SMEM(live_states.shape, jnp.int32),
+                pltpu.SMEM(kept.shape, jnp.int32),
+                pltpu.VMEM(start.shape, jnp.int32),
+                pltpu.VMEM((slots, rows, keep), F32),
+                pltpu.VMEM((slots, keep, part_cols), F32),
                 pltpu.VMEM((slots, rows, states), BF16),
                 pltpu.VMEM((rows * row_count, states), BF16),
-                pltpu.VMEM((states, cols), BF16),
-                pltpu.VMEM((8, 128), BF16),
+                pltpu.VMEM((slots, states, cols), BF16),
                 pltpu.VMEM((2, block, terms * block), BF16),
                 pltpu.VMEM((2, terms * block, block), BF16),
                 pltpu.VMEM((bond, rows * row_count), BF16),
@@ -479,13 +487,13 @@
                 pltpu.VMEM((slots, bond, keep), BF16),
                 pltpu.VMEM((bond, keep), BF16),
                 pltpu.VMEM((slots, bond, keep), BF16),
-                pltpu.VMEM((slots + 2 * steps, 8, keep), F32),
-                dma((2,)),
+                pltpu.VMEM((peers, 1, keep), F32),
+                dma((7 + slots,)),
                 dma((slots, PIECES)), dma((slots, PIECES)),
                 dma((mates - 1, slots, PIECES)), dma((mates - 1, slots, PIECES)),
-                dma((coef_copies,)), dma((coef_copies,)),
+                dma((coef_copies, PIECES)), dma((coef_copies, PIECES)),
                 dma((slots - 1,)), dma((slots - 1,)),
-                dma((slots - 1 + steps,)), dma((slots - 1 + steps,)),
+                dma((peers,)), dma((peers,)),
             ],
             compiler_params=pltpu.CompilerParams(
                 collective_id=0, has_side_effects=True, vmem_limit_bytes=56 * 2**20

time: 63.4 us -> 54.7 us (0.86)
  Pallas kernels: 59.4 us -> 51.2 us
    pallas_call x1, Pallas kernels: 59.4 us -> 51.2 us  [on_device(): pl.pallas_call(functools.partial(gate_kernel, row_count, sec_count), out_...]
where the time goes in v2:
time: 54.7 us; the launch traced here: 54.5 us
  Pallas kernels  51.2 us (94%)
  local copies, waits for them, and re-layouts  2.72 us (5%)
  between operations  0.65 us (1%)
    pallas_call x1, Pallas kernels, on_device(): pl.pallas_call(functools.partial(gate_kernel, row_count, sec_count), out_...  51.2 us
    unnamed x4, local copies, waits for them, and re-layouts  2.72 us

profile of v2, /device:TPU:0, one launch (start us, length us, event | category | flops | bytes accessed | tf_op | source)
XLA Modules:
  0.0 54.5 jit_solution(1968196999050827144)
XLA Ops:
  0.6 51.2 %shard_map.95 = (f32[2,512,128]{2,1,0:T(8,128)}, f32[2,128,512]{2,1,0:T(8,128)}) custom-call(bf16[2,512,128]{2,1,0:T(8,128)(2,1)} %left_hbm.1, bf16[2,128,2048]{2,1,0:T(8,128)(2,1)} %right_hbm.1, f32[4,16,16]{2,1,0:T(8,128)} %lops_hbm.1, f32[4,16,16]{2,1,0:T(8,128)} %rops_hbm.1, s32[16]{0:T(128)} %charges_hbm.1, s32[16]{0:T(128)} %live_hbm.1, s32[16]{0:T(128)} %kept_hbm.1, ...), custom_call_target="tpu_custom_call" | custom-call | tf_op jit(solution)/shard_map/pallas_call | solution.py:453
  51.8 0.0 copy-start
  51.8 1.9 %copy.12 = f32[2,512,128]{2,1,0:T(8,128)} copy(f32[2,512,128]{2,1,0:T(8,128)} %get-tuple-element.4) | data formatting | bytes 1048576
  53.7 0.0 copy-done
  53.7 0.8 %copy.13 = f32[2,128,512]{2,1,0:T(8,128)} copy(f32[2,128,512]{2,1,0:T(8,128)S(1)} %copy-done) | data formatting | bytes 1048576
Async XLA Ops:
  51.8 1.9 %copy-start = (f32[2,128,512]{2,1,0:T(8,128)S(1)}, f32[2,128,512]{2,1,0:T(8,128)}, u32[]{:S(2)}) copy-start(f32[2,128,512]{2,1,0:T(8,128)} %get-tuple-element.5) | copy-start | bytes 1572868

commit v3 on v2

--- a/solution.py
+++ b/solution.py
@@ -12,9 +12,10 @@
 F32, BF16 = jnp.float32, jnp.bfloat16
 chemical = 0.4
 ITERS = 2
-PANEL = 16
-CHUNKS = 2
-PIECES = 2
+PANEL = 32
+TILE = 8
+PIECES = 4
+BITS = 2
 VM = pl.BlockSpec(memory_space=pltpu.VMEM)
 SM = pl.BlockSpec(memory_space=pltpu.SMEM)
 ANY = pl.BlockSpec(memory_space=pl.ANY)
@@ -61,6 +62,12 @@
     ah, al = split2(a)
     bh, bl = split2(b)
     return nt(jnp.concatenate([ah, al, ah], axis=1), jnp.concatenate([bh, bh, bl], axis=1))
+
+
+def tn3(a, b):
+    ah, al = split2(a)
+    bh, bl = split2(b)
+    return tn(jnp.concatenate([ah, al, ah], axis=0), jnp.concatenate([bh, bh, bl], axis=0))
 
 
 def iota(shape, dim):
@@ -78,43 +85,67 @@
     return out
 
 
+def eliminate_panel(x, base):
+    size = x.shape[1]
+    tiles = PANEL // TILE
+    sub, lane = iota((TILE, size), 0), iota((TILE, size), 1)
+    inside = (lane >= base) & (lane < base + PANEL)
+    cols = [
+        {
+            h: jnp.broadcast_to(x[h * TILE : (h + 1) * TILE, base + c : base + c + 1], (TILE, size))
+            for h in range(c // TILE, tiles)
+        }
+        for c in range(PANEL)
+    ]
+    rows = [
+        jnp.where(inside, (lane - (base + h * TILE) == sub).astype(F32), x[h * TILE : (h + 1) * TILE])
+        for h in range(tiles)
+    ]
+    for j in range(0, PANEL, 2):
+        own, q = j // TILE, j % TILE
+        first, second = cols[j], cols[j + 1]
+        a, b, d = first[own][q : q + 1], first[own][q + 1 : q + 2], second[own][q + 1 : q + 2]
+        root = lax.rsqrt(a * d - b * b)
+        inverse = root * root
+        aa, bb, dd = a * inverse, b * inverse, d * inverse
+        w1 = {h: first[h] * dd - second[h] * bb for h in range(own, tiles)}
+        w2 = {h: second[h] * aa - first[h] * bb for h in range(own, tiles)}
+        for i in range(j + 2, PANEL):
+            at, r = i // TILE, i % TILE
+            s1, s2 = first[at][r : r + 1], second[at][r : r + 1]
+            cols[i] = {h: cols[i][h] - w1[h] * s1 - w2[h] * s2 for h in range(at, tiles)}
+        scale = lax.rsqrt(a)
+        x1, x2 = rows[own][q : q + 1], rows[own][q + 1 : q + 2]
+        for h in range(own + 1, tiles):
+            rows[h] = rows[h] - w1[h] * x1 - w2[h] * x2
+        later = rows[own]
+        if q + 2 < TILE:
+            later = later - jnp.where(sub > q + 1, w1[own], 0.0) * x1 - jnp.where(sub > q + 1, w2[own], 0.0) * x2
+        top = x1 * scale
+        bottom = (x2 - x1 * (b * scale * scale)) * (a * scale * root)
+        rows[own] = jnp.where(sub == q, top, jnp.where(sub == q + 1, bottom, later))
+    return jnp.concatenate(rows, axis=0)
+
+
 def inverse_factor(gram, s_ref, t_ref):
     size = gram.shape[0]
     s_ref[...] = gram
-    t_ref[...] = (iota((size, size), 0) == iota((size, size), 1)).astype(F32)
-    sub = iota((PANEL, size), 0)
     lane = iota((PANEL, size), 1)
-
-    def panel(p, carry):
-        base = pl.multiple_of(p * PANEL, PANEL)
-        upper = s_ref[pl.ds(base, PANEL), :]
-        lower = t_ref[pl.ds(base, PANEL), :]
-        turned = pltpu.roll(upper, lax.rem(size - base, size), 1)
-        cols = [jnp.broadcast_to(turned[:, c : c + 1], (PANEL, size)) for c in range(PANEL)]
-        for j in range(PANEL):
-            scale = lax.rsqrt(cols[j][j : j + 1, :])
-            below = jnp.where(sub > j, cols[j] * scale, 0.0)
-            at_j = sub == j
-
-            def eliminate(x):
-                pivot = x[j : j + 1, :] * scale
-                return jnp.where(at_j, pivot, x - below * pivot)
-
-            upper, lower = eliminate(upper), eliminate(lower)
-            cols = [eliminate(c) if i > j else c for i, c in enumerate(cols)]
-        t_ref[pl.ds(base, PANEL), :] = lower
-        u3, l3 = split3(upper), split3(lower)
-        later = lane >= base + PANEL
-        m3 = [jnp.where(later, x.astype(F32), 0.0).astype(BF16) for x in u3]
+    for base in range(0, size, PANEL):
+        after = base + PANEL
+        x = eliminate_panel(s_ref[base:after, :], base)
+        t_ref[base:after, :] = jnp.where(lane < after, x, 0.0)
+        if after == size:
+            break
+        parts = split3(x)
+        masked = [jnp.where(lane >= after, y.astype(F32), 0.0).astype(BF16) for y in parts]
         pairs = ((0, 0), (0, 1), (1, 0), (1, 1), (0, 2), (2, 0))
-        lhs = jnp.concatenate([m3[i] for i, _ in pairs], axis=0)
-        rhs = jnp.concatenate([jnp.concatenate([u3[k], l3[k]], axis=1) for _, k in pairs], axis=0)
-        change = tn(lhs, rhs)
-        s_ref[...] = s_ref[...] - change[:, :size]
-        t_ref[...] = t_ref[...] - change[:, size:]
-        return carry
-
-    lax.fori_loop(0, size // PANEL, panel, 0)
+        change = tn(
+            jnp.concatenate([masked[i] for i, _ in pairs], axis=0),
+            jnp.concatenate([parts[k] for _, k in pairs], axis=0),
+        )
+        inside = (lane[0:1] >= base) & (lane[0:1] < after)
+        s_ref[after:, :] = jnp.where(inside, 0.0, s_ref[after:, :]) - change[after:, :]
 
 
 def gate_kernel(
@@ -226,17 +257,38 @@
     lax.fori_loop(0, states // group, right_chunk, 0)
     gbh_ref[...], gbl_ref[...] = split2(nt(b_ref[...], b_ref[...]))
 
-    def gate_left(part, first, limit, store):
-        part = jnp.where(iota((block, states), 0) + first < limit, part.astype(F32), 0.0)
-        turned = part.T.astype(BF16)
+    def gate_left(parts, firsts, limit, store):
+        parts = [
+            jnp.where(iota(part.shape, 0) + first < limit, part.astype(F32), 0.0)
+            for part, first in zip(parts, firsts)
+        ]
+        turned = jnp.concatenate(parts, axis=0).T.astype(BF16)
         out = nn(turned, kl_ref[0]) + nn(turned, kl_ref[1])
         for t in range(terms):
             store(t, out[:, t * block : (t + 1) * block].astype(BF16))
 
+    def own_chunk(c, carry):
+        t = c // (rows // block)
+        q = lax.rem(c, rows // block)
+        first = pl.multiple_of(q * block, block)
+
+        def store(term, value):
+            own_ref[t, term * states : (term + 1) * states, pl.ds(first, block)] = value
+
+        owner = sec * slots + t
+        gate_left(
+            [lown[t, pl.ds(first, block), :]], [row * rows + first], live_ref[owner] * site, store
+        )
+        return carry
+
+    lax.fori_loop(0, slots * (rows // block), own_chunk, 0)
+
     limit = live_ref[mirror] * site
     forwarded = []
-    for k in range(PIECES):
-        arrived = []
+    ready = block // piece
+    span = row_count * piece
+    def arrive(k):
+        owners = []
         for t in range(slots):
             owner = slot_row(t)
             place = lrecv.at[rows_at(owner, k), :]
@@ -248,41 +300,56 @@
                 )
                 copy.start()
                 forwarded.append(copy)
-            arrived.append((owner, None))
+            owners.append(owner)
+        return owners
+
+    def arrive_from_mates(k):
+        owners = []
         for d in range(1, mates):
             for t in range(slots):
                 owner = t * mates + other_mate(mates - d)
                 place = lrecv.at[rows_at(owner, k), :]
-                arrived.append((owner, remote(
+                remote(
                     place, place, fsend.at[d - 1, t, k], fget.at[d - 1, t, k],
                     (sec, slot * mates + other_mate(mates - d)),
-                )))
-        for index, (owner, copy) in enumerate(arrived):
-            if copy is not None:
-                copy.wait_recv()
-            for q in range(piece // block):
-                column = ((k * row_count + index) * (piece // block) + q) * block
-
-                def store(t, value):
-                    at_ref[t * states : (t + 1) * states, column : column + block] = value
-
-                first = owner * rows + k * piece + q * block
-                gate_left(lrecv[pl.ds(pl.multiple_of(first, block), block), :], first, limit, store)
-        span = row_count * piece
-        gram = nt(at_ref[:, k * span : (k + 1) * span], at_ref[:, k * span : (k + 1) * span])
-        ga_ref[...] = gram if k == 0 else ga_ref[...] + gram
-    gah_ref[...], gal_ref[...] = split2(ga_ref[...])
+                ).wait_recv()
+                owners.append(owner)
+        return owners
+
+    def gate_pieces(owners, k, column):
+        for index in range(0, len(owners), ready):
+            firsts = [owner * rows + k * piece for owner in owners[index : index + ready]]
+            place = column + index * piece
+
+            def store(t, value):
+                at_ref[t * states : (t + 1) * states, place : place + block] = value
+
+            gate_left(
+                [lrecv[pl.ds(pl.multiple_of(first, piece), piece), :] for first in firsts],
+                firsts, limit, store,
+            )
+
+    gram = None
+    for k in range(PIECES + 1):
+        if k < PIECES:
+            gate_pieces(arrive(k), k, k * span)
+        if k:
+            gate_pieces(arrive_from_mates(k - 1), k - 1, (k - 1) * span + slots * piece)
+            done = at_ref[:, (k - 1) * span : k * span]
+            gram = nt(done, done) if gram is None else ga_ref[...] + nt(done, done)
+            if k < PIECES:
+                ga_ref[...] = gram
+    gah_ref[...], gal_ref[...] = split2(gram)
     for copy in sent + forwarded:
         copy.wait_send()
 
     weight = jnp.exp(jnp.full((1, states), charges_ref[home], jnp.int32).astype(F32) * (-chemical))
     coef = (iota((bond, keep), 0) == start_ref[pl.ds(mirror, 1), :]).astype(F32)
     for round_index in range(ITERS + 1):
-        if round_index < ITERS:
-            image = presplit_nn((gah_ref[...], gal_ref[...]), coef)
-        else:
-            image = nn(ga_ref[...], coef, HIGHEST)
-        inverse_factor(tn(coef, image, HIGHEST), s_ref, t_ref)
+        image = presplit_nn((gah_ref[...], gal_ref[...]), coef)
+        norm = lax.rsqrt(jnp.sum(coef * image, axis=0, keepdims=True))
+        coef, image = coef * norm, image * norm
+        inverse_factor(tn3(coef, image), s_ref, t_ref)
         if round_index < ITERS:
             image = nt3(image, t_ref[...])
             coef = presplit_nn((gbh_ref[...], gbl_ref[...]), image) * (weight * weight)
@@ -292,7 +359,7 @@
     msend[...] = out.astype(BF16)
 
     part = bond // mates
-    bit = part // PIECES
+    bit = part // BITS
 
     def coef_rows(m, k):
         return pl.ds(pl.multiple_of(m * part + k * bit, bit), bit)
@@ -307,7 +374,7 @@
         copy.start()
         flying.append(copy)
 
-    for k in range(PIECES):
+    for k in range(BITS):
         go(
             csend.at[coef_rows(mate, k), :], coef_at(slot, mate, k), csems.at[0, k], cgets.at[0, k],
             (partner, row),
@@ -324,22 +391,6 @@
                     total_ref.at[0], total_ref.at[index], tsems.at[index], tgets.at[index],
                     (jnp.bitwise_xor(sec, d), slot_row(other_slot(e))),
                 )
-
-    def own_chunk(c, carry):
-        t = c // (rows // block)
-        q = lax.rem(c, rows // block)
-        first = pl.multiple_of(q * block, block)
-
-        def store(term, value):
-            own_ref[t, term * states : (term + 1) * states, pl.ds(first, block)] = value
-
-        owner = sec * slots + t
-        gate_left(
-            lown[t, pl.ds(first, block), :], row * rows + first, live_ref[owner] * site, store
-        )
-        return carry
-
-    lax.fori_loop(0, slots * (rows // block), own_chunk, 0)
 
     part_rows = here * group
     part_cols = cols // row_count
@@ -374,7 +425,7 @@
                 (sec, slot * mates + other_mate(d)),
             )
 
-    for k in range(PIECES):
+    for k in range(BITS):
         flying[k].wait_recv()
         for e in range(1, slots):
             go(
@@ -382,7 +433,8 @@
                 (sec, slot_row(other_slot(e))),
             )
         pass_on(slot, mate, k, slots)
-    for k in range(PIECES):
+    wide = [tn(msend[...], bw_ref[0])]
+    for k in range(BITS):
         for e in range(1, slots):
             t = other_slot(slots - e)
             remote(
@@ -390,7 +442,6 @@
             ).wait_recv()
             pass_on(t, mate, k, slots + e * (mates - 1))
 
-    wide = [tn(msend[...], bw_ref[0])]
     for d in range(1, slots):
         t = other_slot(slots - d)
         remote(
@@ -422,7 +473,7 @@
 
     for e in range(slots):
         t = other_slot(slots - e)
-        for k in range(PIECES):
+        for k in range(BITS):
             for d in range(1, mates):
                 index = slots + e * (mates - 1) + d - 1
                 m = other_mate(mates - d)
@@ -491,7 +542,7 @@
                 dma((7 + slots,)),
                 dma((slots, PIECES)), dma((slots, PIECES)),
                 dma((mates - 1, slots, PIECES)), dma((mates - 1, slots, PIECES)),
-                dma((coef_copies, PIECES)), dma((coef_copies, PIECES)),
+                dma((coef_copies, BITS)), dma((coef_copies, BITS)),
                 dma((slots - 1,)), dma((slots - 1,)),
                 dma((peers,)), dma((peers,)),
             ],

time: 54.7 us -> 48 us (0.88)
  Pallas kernels: 51.2 us -> 44.5 us
    pallas_call x1, Pallas kernels: 51.2 us -> 44.5 us  [on_device(): pl.pallas_call(functools.partial(gate_kernel, row_count, sec_count), out_...]
where the time goes in v3:
time: 48 us; the launch traced here: 47.8 us
  Pallas kernels  44.5 us (93%)
  local copies, waits for them, and re-layouts  2.72 us (6%)
  between operations  0.65 us (1%)
    pallas_call x1, Pallas kernels, on_device(): pl.pallas_call(functools.partial(gate_kernel, row_count, sec_count), out_...  44.5 us
    unnamed x4, local copies, waits for them, and re-layouts  2.72 us

profile of v3, /device:TPU:0, one launch (start us, length us, event | category | flops | bytes accessed | tf_op | source)
XLA Modules:
  0.0 47.8 jit_solution(7841944330411409163)
XLA Ops:
  0.6 44.5 %shard_map.95 = (f32[2,512,128]{2,1,0:T(8,128)}, f32[2,128,512]{2,1,0:T(8,128)}) custom-call(bf16[2,512,128]{2,1,0:T(8,128)(2,1)} %left_hbm.1, bf16[2,128,2048]{2,1,0:T(8,128)(2,1)} %right_hbm.1, f32[4,16,16]{2,1,0:T(8,128)} %lops_hbm.1, f32[4,16,16]{2,1,0:T(8,128)} %rops_hbm.1, s32[16]{0:T(128)} %charges_hbm.1, s32[16]{0:T(128)} %live_hbm.1, s32[16]{0:T(128)} %kept_hbm.1, ...), custom_call_target="tpu_custom_call" | custom-call | tf_op jit(solution)/shard_map/pallas_call | solution.py:504
  45.1 0.0 copy-start
  45.1 1.9 %copy.12 = f32[2,512,128]{2,1,0:T(8,128)} copy(f32[2,512,128]{2,1,0:T(8,128)} %get-tuple-element.4) | data formatting | bytes 1048576
  47.0 0.0 copy-done
  47.0 0.8 %copy.13 = f32[2,128,512]{2,1,0:T(8,128)} copy(f32[2,128,512]{2,1,0:T(8,128)S(1)} %copy-done) | data formatting | bytes 1048576
Async XLA Ops:
  45.1 1.9 %copy-start = (f32[2,128,512]{2,1,0:T(8,128)S(1)}, f32[2,128,512]{2,1,0:T(8,128)}, u32[]{:S(2)}) copy-start(f32[2,128,512]{2,1,0:T(8,128)} %get-tuple-element.5) | copy-start | bytes 1572868

commit v4 on v3

--- a/solution.py
+++ b/solution.py
@@ -14,6 +14,7 @@
 ITERS = 2
 PANEL = 32
 TILE = 8
+RING = 4
 PIECES = 4
 BITS = 2
 VM = pl.BlockSpec(memory_space=pltpu.VMEM)
@@ -85,7 +86,7 @@
     return out
 
 
-def eliminate_panel(x, base):
+def eliminate_panel(x, base, ring_ref):
     size = x.shape[1]
     tiles = PANEL // TILE
     sub, lane = iota((TILE, size), 0), iota((TILE, size), 1)
@@ -105,6 +106,10 @@
         own, q = j // TILE, j % TILE
         first, second = cols[j], cols[j + 1]
         a, b, d = first[own][q : q + 1], first[own][q + 1 : q + 2], second[own][q + 1 : q + 2]
+        held = j // 2 % RING
+        for h in range(own, tiles):
+            ring_ref[held, 0, h * TILE : (h + 1) * TILE, :] = first[h]
+            ring_ref[held, 1, h * TILE : (h + 1) * TILE, :] = second[h]
         root = lax.rsqrt(a * d - b * b)
         inverse = root * root
         aa, bb, dd = a * inverse, b * inverse, d * inverse
@@ -112,7 +117,10 @@
         w2 = {h: second[h] * aa - first[h] * bb for h in range(own, tiles)}
         for i in range(j + 2, PANEL):
             at, r = i // TILE, i % TILE
-            s1, s2 = first[at][r : r + 1], second[at][r : r + 1]
+            if i < j + 4:
+                s1, s2 = first[at][r : r + 1], second[at][r : r + 1]
+            else:
+                s1, s2 = [ring_ref[held, n, pl.ds(i, TILE, stride=0), :] for n in range(2)]
             cols[i] = {h: cols[i][h] - w1[h] * s1 - w2[h] * s2 for h in range(at, tiles)}
         scale = lax.rsqrt(a)
         x1, x2 = rows[own][q : q + 1], rows[own][q + 1 : q + 2]
@@ -127,13 +135,13 @@
     return jnp.concatenate(rows, axis=0)
 
 
-def inverse_factor(gram, s_ref, t_ref):
+def inverse_factor(gram, s_ref, t_ref, ring_ref):
     size = gram.shape[0]
     s_ref[...] = gram
     lane = iota((PANEL, size), 1)
     for base in range(0, size, PANEL):
         after = base + PANEL
-        x = eliminate_panel(s_ref[base:after, :], base)
+        x = eliminate_panel(s_ref[base:after, :], base, ring_ref)
         t_ref[base:after, :] = jnp.where(lane < after, x, 0.0)
         if after == size:
             break
@@ -148,11 +156,16 @@
         s_ref[after:, :] = jnp.where(inside, 0.0, s_ref[after:, :]) - change[after:, :]
 
 
+def low_part(count):
+    bits = count.bit_length() - 1
+    return 1 << (bits // 2)
+
+
 def gate_kernel(
     row_count, sec_count, left_hbm, right_hbm, lops_hbm, rops_hbm, charges_hbm, live_hbm, kept_hbm,
     start_hbm, u_hbm, w_hbm, lops_ref, rops_ref, charges_ref, live_ref, kept_ref, start_ref, u_out, w_out,
     lown, lrecv, rown, kl_ref, kr_ref, at_ref, own_ref, b_ref, bw_ref, ga_ref, gah_ref, gal_ref,
-    gbh_ref, gbl_ref, s_ref, t_ref, csend, crecv, msend, mrecv, total_ref,
+    gbh_ref, gbl_ref, s_ref, t_ref, ring_ref, csend, crecv, msend, mrecv, total_ref,
     local, lsend, lget, fsend, fget, csems, cgets, msems, mgets, tsems, tgets,
 ):
     slots, rows, states = left_hbm.shape
@@ -185,10 +198,14 @@
         return lax.rem(mate + d, mates)
 
     greeted = [(sec, slot * mates + other_mate(d)) for d in range(1, mates)]
+    near_count = low_part(sec_count)
+    far_count = sec_count // near_count
     greeted += [
         (jnp.bitwise_xor(sec, d), slot_row(other_slot(e)))
-        for d in range(sec_count) for e in range(slots) if d or e
+        for d in range(near_count) for e in range(slots) if d or e
     ]
+    greeted += [(jnp.bitwise_xor(sec, h * near_count), row) for h in range(1, far_count)]
+    greeted += [(partner, slot_row(other_slot(e))) for e in range(1, slots)]
     barrier = pltpu.get_barrier_semaphore()
     for device in greeted:
         pl.semaphore_signal(barrier, inc=1, device_id=device, device_id_type=MESH)
@@ -349,14 +366,12 @@
         image = presplit_nn((gah_ref[...], gal_ref[...]), coef)
         norm = lax.rsqrt(jnp.sum(coef * image, axis=0, keepdims=True))
         coef, image = coef * norm, image * norm
-        inverse_factor(tn3(coef, image), s_ref, t_ref)
+        inverse_factor(tn3(coef, image), s_ref, t_ref, ring_ref)
         if round_index < ITERS:
             image = nt3(image, t_ref[...])
             coef = presplit_nn((gbh_ref[...], gbl_ref[...]), image) * (weight * weight)
     kept_here = iota((bond, keep), 1) < kept_ref[home]
     csend[...] = jnp.where(kept_here, nt3(coef, t_ref[...]), 0.0).astype(BF16)
-    out = jnp.where(kept_here, nt3(image, t_ref[...]) * weight, 0.0)
-    msend[...] = out.astype(BF16)
 
     part = bond // mates
     bit = part // BITS
@@ -366,6 +381,9 @@
 
     def coef_at(t, m, k):
         return crecv.at[t, coef_rows(m, k), :]
+
+    def m_rows(m):
+        return pl.ds(pl.multiple_of(m * part, part), part)
 
     flying = []
 
@@ -374,23 +392,42 @@
         copy.start()
         flying.append(copy)
 
+    out = jnp.where(kept_here, nt3(image, t_ref[...]) * weight, 0.0)
     for k in range(BITS):
         go(
             csend.at[coef_rows(mate, k), :], coef_at(slot, mate, k), csems.at[0, k], cgets.at[0, k],
             (partner, row),
         )
+    msend[...] = out.astype(BF16)
     per = out * presplit_nn((gbh_ref[...], gbl_ref[...]), out)
-    for d in range(1, slots):
-        go(msend, mrecv.at[slot], msems.at[d - 1], mgets.at[d - 1], (sec, slot_row(other_slot(d))))
+    for e in range(1, slots):
+        go(
+            msend.at[m_rows(mate), :], mrecv.at[slot, m_rows(mate), :], msems.at[e - 1], mgets.at[e - 1],
+            (sec, slot_row(other_slot(e))),
+        )
     total_ref[0] = jnp.sum(per, axis=0, keepdims=True)
-    for d in range(sec_count):
-        for e in range(slots):
-            if d or e:
-                index = d * slots + e
-                go(
-                    total_ref.at[0], total_ref.at[index], tsems.at[index], tgets.at[index],
-                    (jnp.bitwise_xor(sec, d), slot_row(other_slot(e))),
-                )
+
+    def add_totals(start, peers):
+        for n, device in enumerate(peers):
+            index = start + 1 + n
+            go(total_ref.at[start], total_ref.at[index], tsems.at[index], tgets.at[index], device)
+
+    def sum_totals(start, peers):
+        summed = total_ref[start]
+        for n, device in enumerate(peers):
+            index = start + 1 + n
+            remote(
+                total_ref.at[start], total_ref.at[index], tsems.at[index], tgets.at[index], device
+            ).wait_recv()
+            summed = summed + total_ref[index]
+        return summed
+
+    near_peers = [
+        (jnp.bitwise_xor(sec, d), slot_row(other_slot(e)))
+        for d in range(near_count) for e in range(slots) if d or e
+    ]
+    far_peers = [(jnp.bitwise_xor(sec, h * near_count), row) for h in range(1, far_count)]
+    add_totals(0, near_peers)
 
     part_rows = here * group
     part_cols = cols // row_count
@@ -425,6 +462,9 @@
                 (sec, slot * mates + other_mate(d)),
             )
 
+    far_start = len(near_peers) + 1
+    total_ref[far_start] = sum_totals(0, near_peers)
+    add_totals(far_start, far_peers)
     for k in range(BITS):
         flying[k].wait_recv()
         for e in range(1, slots):
@@ -433,6 +473,14 @@
                 (sec, slot_row(other_slot(e))),
             )
         pass_on(slot, mate, k, slots)
+    number = slots - 1
+    for e in range(1, slots):
+        t = other_slot(slots - e)
+        place = mrecv.at[t, m_rows(mate), :]
+        remote(place, place, msems.at[e - 1], mgets.at[e - 1], (sec, slot_row(t))).wait_recv()
+        for d in range(1, mates):
+            go(place, place, msems.at[number], mgets.at[number], (sec, slot * mates + other_mate(d)))
+            number += 1
     wide = [tn(msend[...], bw_ref[0])]
     for k in range(BITS):
         for e in range(1, slots):
@@ -441,24 +489,16 @@
                 coef_at(t, mate, k), coef_at(t, mate, k), csems.at[e, k], cgets.at[e, k], (sec, slot_row(t))
             ).wait_recv()
             pass_on(t, mate, k, slots + e * (mates - 1))
-
-    for d in range(1, slots):
-        t = other_slot(slots - d)
-        remote(
-            msend, mrecv.at[t], msems.at[d - 1], mgets.at[d - 1], (sec, slot_row(t))
-        ).wait_recv()
-        wide.append(tn(mrecv[t], bw_ref[slots - d]))
-    summed = total_ref[0]
-    for d in range(sec_count):
-        for e in range(slots):
-            if d or e:
-                index = d * slots + e
-                remote(
-                    total_ref.at[0], total_ref.at[index], tsems.at[index], tgets.at[index],
-                    (jnp.bitwise_xor(sec, d), slot_row(other_slot(slots - e))),
-                ).wait_recv()
-                summed = summed + total_ref[index]
-    scale = 1.0 / jnp.sqrt(jnp.sum(summed, keepdims=True))
+    number = slots - 1
+    for e in range(1, slots):
+        t = other_slot(slots - e)
+        for d in range(1, mates):
+            m = other_mate(mates - d)
+            place = mrecv.at[t, m_rows(m), :]
+            remote(place, place, msems.at[number], mgets.at[number], (sec, slot * mates + m)).wait_recv()
+            number += 1
+        wide.append(tn(mrecv[t], bw_ref[slots - e]))
+    scale = 1.0 / jnp.sqrt(jnp.sum(sum_totals(far_start, far_peers), keepdims=True))
     leaving = []
 
     def leave(source, target):
@@ -499,7 +539,9 @@
         block, mates = 256, row_count // slots
         part_cols = cols // row_count
         coef_copies = slots + slots * (mates - 1)
-        peers = slots * sec_count
+        m_copies = (slots - 1) * mates
+        near_count = low_part(sec_count)
+        peers = slots * near_count + sec_count // near_count
         dma = pltpu.SemaphoreType.DMA
         return pl.pallas_call(
             functools.partial(gate_kernel, row_count, sec_count),
@@ -534,6 +576,7 @@
                 pltpu.VMEM((bond, bond), BF16),
                 pltpu.VMEM((keep, keep), F32),
                 pltpu.VMEM((keep, keep), F32),
+                pltpu.VMEM((RING, 2, PANEL, keep), F32),
                 pltpu.VMEM((bond, keep), BF16),
                 pltpu.VMEM((slots, bond, keep), BF16),
                 pltpu.VMEM((bond, keep), BF16),
@@ -543,7 +586,7 @@
                 dma((slots, PIECES)), dma((slots, PIECES)),
                 dma((mates - 1, slots, PIECES)), dma((mates - 1, slots, PIECES)),
                 dma((coef_copies, BITS)), dma((coef_copies, BITS)),
-                dma((slots - 1,)), dma((slots - 1,)),
+                dma((m_copies,)), dma((m_copies,)),
                 dma((peers,)), dma((peers,)),
             ],
             compiler_params=pltpu.CompilerParams(

time: 48 us -> 46.4 us (0.967)
  Pallas kernels: 44.5 us -> 42.9 us
    pallas_call x1, Pallas kernels: 44.5 us -> 42.9 us  [on_device(): pl.pallas_call(functools.partial(gate_kernel, row_count, sec_count), out_...]
where the time goes in v4:
time: 46.4 us; the launch traced here: 46.3 us
  Pallas kernels  42.9 us (92%)
  local copies, waits for them, and re-layouts  2.72 us (6%)
  between operations  0.65 us (1%)
    pallas_call x1, Pallas kernels, on_device(): pl.pallas_call(functools.partial(gate_kernel, row_count, sec_count), out_...  42.9 us
    unnamed x4, local copies, waits for them, and re-layouts  2.72 us

profile of v4, /device:TPU:0, one launch (start us, length us, event | category | flops | bytes accessed | tf_op | source)
XLA Modules:
  0.0 46.3 jit_solution(2315057589874796907)
XLA Ops:
  0.6 42.9 %shard_map.95 = (f32[2,512,128]{2,1,0:T(8,128)}, f32[2,128,512]{2,1,0:T(8,128)}) custom-call(bf16[2,512,128]{2,1,0:T(8,128)(2,1)} %left_hbm.1, bf16[2,128,2048]{2,1,0:T(8,128)(2,1)} %right_hbm.1, f32[4,16,16]{2,1,0:T(8,128)} %lops_hbm.1, f32[4,16,16]{2,1,0:T(8,128)} %rops_hbm.1, s32[16]{0:T(128)} %charges_hbm.1, s32[16]{0:T(128)} %live_hbm.1, s32[16]{0:T(128)} %kept_hbm.1, ...), custom_call_target="tpu_custom_call" | custom-call | tf_op jit(solution)/shard_map/pallas_call | solution.py:546
  43.5 0.0 copy-start
  43.5 1.9 %copy.12 = f32[2,512,128]{2,1,0:T(8,128)} copy(f32[2,512,128]{2,1,0:T(8,128)} %get-tuple-element.4) | data formatting | bytes 1048576
  45.5 0.0 copy-done
  45.5 0.8 %copy.13 = f32[2,128,512]{2,1,0:T(8,128)} copy(f32[2,128,512]{2,1,0:T(8,128)S(1)} %copy-done) | data formatting | bytes 1048576
Async XLA Ops:
  43.5 1.9 %copy-start = (f32[2,128,512]{2,1,0:T(8,128)S(1)}, f32[2,128,512]{2,1,0:T(8,128)}, u32[]{:S(2)}) copy-start(f32[2,128,512]{2,1,0:T(8,128)} %get-tuple-element.5) | copy-start | bytes 1572868

commit v5 on v4

--- a/solution.py
+++ b/solution.py
@@ -20,6 +20,7 @@
 VM = pl.BlockSpec(memory_space=pltpu.VMEM)
 SM = pl.BlockSpec(memory_space=pltpu.SMEM)
 ANY = pl.BlockSpec(memory_space=pl.ANY)
+HBM = pl.BlockSpec(memory_space=pltpu.HBM)
 
 
 def nn(a, b, precision=None):
@@ -163,7 +164,7 @@
 
 def gate_kernel(
     row_count, sec_count, left_hbm, right_hbm, lops_hbm, rops_hbm, charges_hbm, live_hbm, kept_hbm,
-    start_hbm, u_hbm, w_hbm, lops_ref, rops_ref, charges_ref, live_ref, kept_ref, start_ref, u_out, w_out,
+    start_hbm, u_out, w_out, lops_ref, rops_ref, charges_ref, live_ref, kept_ref, start_ref,
     lown, lrecv, rown, kl_ref, kr_ref, at_ref, own_ref, b_ref, bw_ref, ga_ref, gah_ref, gal_ref,
     gbh_ref, gbl_ref, s_ref, t_ref, ring_ref, csend, crecv, msend, mrecv, total_ref,
     local, lsend, lget, fsend, fget, csems, cgets, msems, mgets, tsems, tgets,
@@ -499,17 +500,8 @@
             number += 1
         wide.append(tn(mrecv[t], bw_ref[slots - e]))
     scale = 1.0 / jnp.sqrt(jnp.sum(sum_totals(far_start, far_peers), keepdims=True))
-    leaving = []
-
-    def leave(source, target):
-        copy = pltpu.make_async_copy(source, target, local.at[len(leaving)])
-        copy.start()
-        leaving.append(copy)
-
     for d in range(slots):
-        t = other_slot(slots - d)
-        w_out[d] = wide[d] * scale
-        leave(w_out.at[d], w_hbm.at[t])
+        w_out[other_slot(slots - d)] = wide[d] * scale
 
     for e in range(slots):
         t = other_slot(slots - e)
@@ -521,12 +513,9 @@
                     coef_at(t, m, k), coef_at(t, m, k), csems.at[index, k], cgets.at[index, k],
                     (sec, slot * mates + m),
                 ).wait_recv()
-        u_out[e] = tn(own_ref[t], crecv[t])
-        leave(u_out.at[e], u_hbm.at[t])
+        u_out[t] = tn(own_ref[t], crecv[t])
     for copy in flying:
         copy.wait_send()
-    for copy in leaving:
-        copy.wait()
 
 
 def solution(mesh):
@@ -543,14 +532,12 @@
         near_count = low_part(sec_count)
         peers = slots * near_count + sec_count // near_count
         dma = pltpu.SemaphoreType.DMA
+        u_shape, w_shape = (slots, rows, keep), (slots, keep, part_cols)
         return pl.pallas_call(
             functools.partial(gate_kernel, row_count, sec_count),
-            out_shape=(
-                jax.ShapeDtypeStruct((slots, rows, keep), F32),
-                jax.ShapeDtypeStruct((slots, keep, part_cols), F32),
-            ),
-            in_specs=[ANY] * 8,
-            out_specs=[ANY] * 2,
+            out_shape=(pltpu.VMEM(u_shape, F32), pltpu.VMEM(w_shape, F32)),
+            in_specs=[HBM] * 8,
+            out_specs=[VM] * 2,
             scratch_shapes=[
                 pltpu.VMEM(left_ops.shape, F32),
                 pltpu.VMEM(right_ops.shape, F32),
@@ -558,8 +545,6 @@
                 pltpu.SMEM(live_states.shape, jnp.int32),
                 pltpu.SMEM(kept.shape, jnp.int32),
                 pltpu.VMEM(start.shape, jnp.int32),
-                pltpu.VMEM((slots, rows, keep), F32),
-                pltpu.VMEM((slots, keep, part_cols), F32),
                 pltpu.VMEM((slots, rows, states), BF16),
                 pltpu.VMEM((rows * row_count, states), BF16),
                 pltpu.VMEM((slots, states, cols), BF16),
@@ -590,10 +575,9 @@
                 dma((peers,)), dma((peers,)),
             ],
             compiler_params=pltpu.CompilerParams(
-                collective_id=0, has_side_effects=True, vmem_limit_bytes=56 * 2**20
+                collective_id=0, has_side_effects=True, vmem_limit_bytes=62 * 2**20
             ),
         )(left_block, right_block, left_ops, right_ops, charges, live_states, kept, start)
-
     return jax.shard_map(
         on_device,
         mesh=mesh,

time: 46.4 us -> 44.6 us (0.961)
  local copies, waits for them, and re-layouts: 2.72 us -> 1.59 us
  Pallas kernels: 42.9 us -> 42.2 us
    unnamed x4 -> x2, local copies, waits for them, and re-layouts: 2.72 us -> 1.59 us
    pallas_call x1, Pallas kernels: 42.9 us -> 42.2 us  [on_device(): pl.pallas_call(functools.partial(gate_kernel, row_count, sec_count), out_...]
where the time goes in v5:
time: 44.6 us; the launch traced here: 44.4 us
  Pallas kernels  42.2 us (95%)
  local copies, waits for them, and re-layouts  1.59 us (4%)
  between operations  0.64 us (1%)
    pallas_call x1, Pallas kernels, on_device(): pl.pallas_call(functools.partial(gate_kernel, row_count, sec_count), out_...  42.2 us
    unnamed x2, local copies, waits for them, and re-layouts  1.59 us

profile of v5, /device:TPU:0, one launch (start us, length us, event | category | flops | bytes accessed | tf_op | source)
XLA Modules:
  0.0 44.4 jit_solution(11932532277974982433)
XLA Ops:
  0.6 42.2 %shard_map.95 = (f32[2,512,128]{2,1,0:T(8,128)S(1)}, f32[2,128,512]{2,1,0:T(8,128)S(1)}) custom-call(bf16[2,512,128]{2,1,0:T(8,128)(2,1)} %left_hbm.1, bf16[2,128,2048]{2,1,0:T(8,128)(2,1)} %right_hbm.1, f32[4,16,16]{2,1,0:T(8,128)} %lops_hbm.1, f32[4,16,16]{2,1,0:T(8,128)} %rops_hbm.1, s32[16]{0:T(128)} %charges_hbm.1, s32[16]{0:T(128)} %live_hbm.1, ...), custom_call_target="tpu_custom_call" | custom-call | tf_op jit(solution)/shard_map/pallas_call | solution.py:536
  42.9 0.8 %copy.12 = f32[2,512,128]{2,1,0:T(8,128)} copy(f32[2,512,128]{2,1,0:T(8,128)S(1)} %get-tuple-element.2) | data formatting | bytes 1048576
  43.7 0.8 %copy.13 = f32[2,128,512]{2,1,0:T(8,128)} copy(f32[2,128,512]{2,1,0:T(8,128)S(1)} %get-tuple-element.3) | data formatting | bytes 1048576

commit v6 on v5

--- a/solution.py
+++ b/solution.py
@@ -166,7 +166,7 @@
     row_count, sec_count, left_hbm, right_hbm, lops_hbm, rops_hbm, charges_hbm, live_hbm, kept_hbm,
     start_hbm, u_out, w_out, lops_ref, rops_ref, charges_ref, live_ref, kept_ref, start_ref,
     lown, lrecv, rown, kl_ref, kr_ref, at_ref, own_ref, b_ref, bw_ref, ga_ref, gah_ref, gal_ref,
-    gbh_ref, gbl_ref, s_ref, t_ref, ring_ref, csend, crecv, msend, mrecv, total_ref,
+    gbh_ref, gbl_ref, s_ref, t_ref, ring_ref, coef_ref, csend, crecv, msend, mrecv, total_ref,
     local, lsend, lget, fsend, fget, csems, cgets, msems, mgets, tsems, tgets,
 ):
     slots, rows, states = left_hbm.shape
@@ -291,7 +291,7 @@
         first = pl.multiple_of(q * block, block)
 
         def store(term, value):
-            own_ref[t, term * states : (term + 1) * states, pl.ds(first, block)] = value
+            own_ref[t, pl.ds(first, block), term * states : (term + 1) * states] = value.T
 
         owner = sec * slots + t
         gate_left(
@@ -372,8 +372,6 @@
             image = nt3(image, t_ref[...])
             coef = presplit_nn((gbh_ref[...], gbl_ref[...]), image) * (weight * weight)
     kept_here = iota((bond, keep), 1) < kept_ref[home]
-    csend[...] = jnp.where(kept_here, nt3(coef, t_ref[...]), 0.0).astype(BF16)
-
     part = bond // mates
     bit = part // BITS
 
@@ -385,6 +383,10 @@
 
     def m_rows(m):
         return pl.ds(pl.multiple_of(m * part, part), part)
+
+    coef_ref[...] = coef
+    kept_part = iota((part, keep), 1) < kept_ref[home]
+    csend[...] = jnp.where(kept_part, nt3(coef_ref[m_rows(mate), :], t_ref[...]), 0.0).astype(BF16)
 
     flying = []
 
@@ -393,19 +395,14 @@
         copy.start()
         flying.append(copy)
 
-    out = jnp.where(kept_here, nt3(image, t_ref[...]) * weight, 0.0)
     for k in range(BITS):
         go(
-            csend.at[coef_rows(mate, k), :], coef_at(slot, mate, k), csems.at[0, k], cgets.at[0, k],
+            csend.at[pl.ds(k * bit, bit), :], coef_at(slot, mate, k), csems.at[0, k], cgets.at[0, k],
             (partner, row),
         )
+    out = jnp.where(kept_here, nt3(image, t_ref[...]) * weight, 0.0)
     msend[...] = out.astype(BF16)
     per = out * presplit_nn((gbh_ref[...], gbl_ref[...]), out)
-    for e in range(1, slots):
-        go(
-            msend.at[m_rows(mate), :], mrecv.at[slot, m_rows(mate), :], msems.at[e - 1], mgets.at[e - 1],
-            (sec, slot_row(other_slot(e))),
-        )
     total_ref[0] = jnp.sum(per, axis=0, keepdims=True)
 
     def add_totals(start, peers):
@@ -429,6 +426,11 @@
     ]
     far_peers = [(jnp.bitwise_xor(sec, h * near_count), row) for h in range(1, far_count)]
     add_totals(0, near_peers)
+    for e in range(1, slots):
+        go(
+            msend.at[m_rows(mate), :], mrecv.at[slot, m_rows(mate), :], msems.at[e - 1], mgets.at[e - 1],
+            (sec, slot_row(other_slot(e))),
+        )
 
     part_rows = here * group
     part_cols = cols // row_count
@@ -464,8 +466,6 @@
             )
 
     far_start = len(near_peers) + 1
-    total_ref[far_start] = sum_totals(0, near_peers)
-    add_totals(far_start, far_peers)
     for k in range(BITS):
         flying[k].wait_recv()
         for e in range(1, slots):
@@ -474,6 +474,9 @@
                 (sec, slot_row(other_slot(e))),
             )
         pass_on(slot, mate, k, slots)
+        if k == 0:
+            total_ref[far_start] = sum_totals(0, near_peers)
+            add_totals(far_start, far_peers)
     number = slots - 1
     for e in range(1, slots):
         t = other_slot(slots - e)
@@ -482,7 +485,20 @@
         for d in range(1, mates):
             go(place, place, msems.at[number], mgets.at[number], (sec, slot * mates + other_mate(d)))
             number += 1
+    def from_mates(e):
+        t = other_slot(slots - e)
+        for k in range(BITS):
+            for d in range(1, mates):
+                index = slots + e * (mates - 1) + d - 1
+                m = other_mate(mates - d)
+                remote(
+                    coef_at(t, m, k), coef_at(t, m, k), csems.at[index, k], cgets.at[index, k],
+                    (sec, slot * mates + m),
+                ).wait_recv()
+
     wide = [tn(msend[...], bw_ref[0])]
+    from_mates(0)
+    u_out[slot] = nn(own_ref[slot], crecv[slot])
     for k in range(BITS):
         for e in range(1, slots):
             t = other_slot(slots - e)
@@ -503,17 +519,10 @@
     for d in range(slots):
         w_out[other_slot(slots - d)] = wide[d] * scale
 
-    for e in range(slots):
+    for e in range(1, slots):
         t = other_slot(slots - e)
-        for k in range(BITS):
-            for d in range(1, mates):
-                index = slots + e * (mates - 1) + d - 1
-                m = other_mate(mates - d)
-                remote(
-                    coef_at(t, m, k), coef_at(t, m, k), csems.at[index, k], cgets.at[index, k],
-                    (sec, slot * mates + m),
-                ).wait_recv()
-        u_out[t] = tn(own_ref[t], crecv[t])
+        from_mates(e)
+        u_out[t] = nn(own_ref[t], crecv[t])
     for copy in flying:
         copy.wait_send()
 
@@ -551,7 +560,7 @@
                 pltpu.VMEM((2, block, terms * block), BF16),
                 pltpu.VMEM((2, terms * block, block), BF16),
                 pltpu.VMEM((bond, rows * row_count), BF16),
-                pltpu.VMEM((slots, bond, rows), BF16),
+                pltpu.VMEM((slots, rows, bond), BF16),
                 pltpu.VMEM((bond, cols), BF16),
                 pltpu.VMEM((slots, bond, part_cols), BF16),
                 pltpu.VMEM((bond, bond), F32),
@@ -562,7 +571,8 @@
                 pltpu.VMEM((keep, keep), F32),
                 pltpu.VMEM((keep, keep), F32),
                 pltpu.VMEM((RING, 2, PANEL, keep), F32),
-                pltpu.VMEM((bond, keep), BF16),
+                pltpu.VMEM((bond, keep), F32),
+                pltpu.VMEM((bond // mates, keep), BF16),
                 pltpu.VMEM((slots, bond, keep), BF16),
                 pltpu.VMEM((bond, keep), BF16),
                 pltpu.VMEM((slots, bond, keep), BF16),

time: 44.6 us -> 43.9 us (0.984)
  Pallas kernels: 42.2 us -> 41.5 us
    pallas_call x1, Pallas kernels: 42.2 us -> 41.5 us  [on_device(): pl.pallas_call(functools.partial(gate_kernel, row_count, sec_count), out_...]
where the time goes in v6:
time: 43.9 us; the launch traced here: 43.8 us
  Pallas kernels  41.5 us (95%)
  local copies, waits for them, and re-layouts  1.59 us (4%)
  between operations  0.64 us (1%)
    pallas_call x1, Pallas kernels, on_device(): pl.pallas_call(functools.partial(gate_kernel, row_count, sec_count), out_...  41.5 us
    unnamed x2, local copies, waits for them, and re-layouts  1.59 us

profile of v6, /device:TPU:0, one launch (start us, length us, event | category | flops | bytes accessed | tf_op | source)
XLA Modules:
  0.0 43.8 jit_solution(4772877378807147152)
XLA Ops:
  0.6 41.5 %shard_map.95 = (f32[2,512,128]{2,1,0:T(8,128)S(1)}, f32[2,128,512]{2,1,0:T(8,128)S(1)}) custom-call(bf16[2,512,128]{2,1,0:T(8,128)(2,1)} %left_hbm.1, bf16[2,128,2048]{2,1,0:T(8,128)(2,1)} %right_hbm.1, f32[4,16,16]{2,1,0:T(8,128)} %lops_hbm.1, f32[4,16,16]{2,1,0:T(8,128)} %rops_hbm.1, s32[16]{0:T(128)} %charges_hbm.1, s32[16]{0:T(128)} %live_hbm.1, ...), custom_call_target="tpu_custom_call" | custom-call | tf_op jit(solution)/shard_map/pallas_call | solution.py:545
  42.2 0.8 %copy.12 = f32[2,512,128]{2,1,0:T(8,128)} copy(f32[2,512,128]{2,1,0:T(8,128)S(1)} %get-tuple-element.2) | data formatting | bytes 1048576
  43.0 0.8 %copy.13 = f32[2,128,512]{2,1,0:T(8,128)} copy(f32[2,128,512]{2,1,0:T(8,128)S(1)} %get-tuple-element.3) | data formatting | bytes 1048576

commit v7 on v6

--- a/solution.py
+++ b/solution.py
@@ -136,12 +136,14 @@
     return jnp.concatenate(rows, axis=0)
 
 
-def inverse_factor(gram, s_ref, t_ref, ring_ref):
+def inverse_factor(gram, s_ref, t_ref, ring_ref, beside=None):
     size = gram.shape[0]
     s_ref[...] = gram
     lane = iota((PANEL, size), 1)
     for base in range(0, size, PANEL):
         after = base + PANEL
+        if beside is not None:
+            beside(base // PANEL)
         x = eliminate_panel(s_ref[base:after, :], base, ring_ref)
         t_ref[base:after, :] = jnp.where(lane < after, x, 0.0)
         if after == size:
@@ -363,14 +365,20 @@
 
     weight = jnp.exp(jnp.full((1, states), charges_ref[home], jnp.int32).astype(F32) * (-chemical))
     coef = (iota((bond, keep), 0) == start_ref[pl.ds(mirror, 1), :]).astype(F32)
+    share = bond * PANEL // keep
     for round_index in range(ITERS + 1):
         image = presplit_nn((gah_ref[...], gal_ref[...]), coef)
         norm = lax.rsqrt(jnp.sum(coef * image, axis=0, keepdims=True))
         coef, image = coef * norm, image * norm
-        inverse_factor(tn3(coef, image), s_ref, t_ref, ring_ref)
-        if round_index < ITERS:
-            image = nt3(image, t_ref[...])
-            coef = presplit_nn((gbh_ref[...], gbl_ref[...]), image) * (weight * weight)
+
+        def following(n):
+            span = pl.ds(n * share, share)
+            coef_ref[span, :] = presplit_nn((gbh_ref[span, :], gbl_ref[span, :]), image)
+
+        last = round_index == ITERS
+        inverse_factor(tn3(coef, image), s_ref, t_ref, ring_ref, None if last else following)
+        if not last:
+            coef = nt3(coef_ref[...], t_ref[...]) * (weight * weight)
     kept_here = iota((bond, keep), 1) < kept_ref[home]
     part = bond // mates
     bit = part // BITS
@@ -499,13 +507,6 @@
     wide = [tn(msend[...], bw_ref[0])]
     from_mates(0)
     u_out[slot] = nn(own_ref[slot], crecv[slot])
-    for k in range(BITS):
-        for e in range(1, slots):
-            t = other_slot(slots - e)
-            remote(
-                coef_at(t, mate, k), coef_at(t, mate, k), csems.at[e, k], cgets.at[e, k], (sec, slot_row(t))
-            ).wait_recv()
-            pass_on(t, mate, k, slots + e * (mates - 1))
     number = slots - 1
     for e in range(1, slots):
         t = other_slot(slots - e)
@@ -515,14 +516,21 @@
             remote(place, place, msems.at[number], mgets.at[number], (sec, slot * mates + m)).wait_recv()
             number += 1
         wide.append(tn(mrecv[t], bw_ref[slots - e]))
-    scale = 1.0 / jnp.sqrt(jnp.sum(sum_totals(far_start, far_peers), keepdims=True))
-    for d in range(slots):
-        w_out[other_slot(slots - d)] = wide[d] * scale
-
+    for k in range(BITS):
+        for e in range(1, slots):
+            t = other_slot(slots - e)
+            remote(
+                coef_at(t, mate, k), coef_at(t, mate, k), csems.at[e, k], cgets.at[e, k], (sec, slot_row(t))
+            ).wait_recv()
+            pass_on(t, mate, k, slots + e * (mates - 1))
     for e in range(1, slots):
         t = other_slot(slots - e)
         from_mates(e)
         u_out[t] = nn(own_ref[t], crecv[t])
+    scale = 1.0 / jnp.sqrt(jnp.sum(sum_totals(far_start, far_peers), keepdims=True))
+    for d in range(slots):
+        w_out[other_slot(slots - d)] = wide[d] * scale
+
     for copy in flying:
         copy.wait_send()
 

time: 43.9 us -> 42.9 us (0.977)
  Pallas kernels: 41.5 us -> 40.5 us
    pallas_call x1, Pallas kernels: 41.5 us -> 40.5 us  [on_device(): pl.pallas_call(functools.partial(gate_kernel, row_count, sec_count), out_...]
where the time goes in v7:
time: 42.9 us; the launch traced here: 42.7 us
  Pallas kernels  40.5 us (94%)
  local copies, waits for them, and re-layouts  1.59 us (4%)
  between operations  0.64 us (1%)
    pallas_call x1, Pallas kernels, on_device(): pl.pallas_call(functools.partial(gate_kernel, row_count, sec_count), out_...  40.5 us
    unnamed x2, local copies, waits for them, and re-layouts  1.59 us

profile of v7, /device:TPU:0, one launch (start us, length us, event | category | flops | bytes accessed | tf_op | source)
XLA Modules:
  0.0 42.7 jit_solution(16702818941185952146)
XLA Ops:
  0.6 40.5 %shard_map.95 = (f32[2,512,128]{2,1,0:T(8,128)S(1)}, f32[2,128,512]{2,1,0:T(8,128)S(1)}) custom-call(bf16[2,512,128]{2,1,0:T(8,128)(2,1)} %left_hbm.1, bf16[2,128,2048]{2,1,0:T(8,128)(2,1)} %right_hbm.1, f32[4,16,16]{2,1,0:T(8,128)} %lops_hbm.1, f32[4,16,16]{2,1,0:T(8,128)} %rops_hbm.1, s32[16]{0:T(128)} %charges_hbm.1, s32[16]{0:T(128)} %live_hbm.1, ...), custom_call_target="tpu_custom_call" | custom-call | tf_op jit(solution)/shard_map/pallas_call | solution.py:553
  41.2 0.8 %copy.12 = f32[2,512,128]{2,1,0:T(8,128)} copy(f32[2,512,128]{2,1,0:T(8,128)S(1)} %get-tuple-element.2) | data formatting | bytes 1048576
  42.0 0.8 %copy.13 = f32[2,128,512]{2,1,0:T(8,128)} copy(f32[2,128,512]{2,1,0:T(8,128)S(1)} %get-tuple-element.3) | data formatting | bytes 1048576

commit v8 on v7

--- a/solution.py
+++ b/solution.py
@@ -277,31 +277,33 @@
     lax.fori_loop(0, states // group, right_chunk, 0)
     gbh_ref[...], gbl_ref[...] = split2(nt(b_ref[...], b_ref[...]))
 
-    def gate_left(parts, firsts, limit, store):
-        parts = [
-            jnp.where(iota(part.shape, 0) + first < limit, part.astype(F32), 0.0)
-            for part, first in zip(parts, firsts)
-        ]
-        turned = jnp.concatenate(parts, axis=0).T.astype(BF16)
+    def gate_left(blocks, limit, store):
+        turned = jnp.concatenate([
+            jnp.concatenate([
+                jnp.where(iota(part.shape, 0) + first < limit, part.astype(F32), 0.0)
+                for part, first in parts
+            ], axis=0).T.astype(BF16)
+            for parts in blocks
+        ], axis=0)
         out = nn(turned, kl_ref[0]) + nn(turned, kl_ref[1])
-        for t in range(terms):
-            store(t, out[:, t * block : (t + 1) * block].astype(BF16))
-
-    def own_chunk(c, carry):
-        t = c // (rows // block)
-        q = lax.rem(c, rows // block)
-        first = pl.multiple_of(q * block, block)
-
-        def store(term, value):
-            own_ref[t, pl.ds(first, block), term * states : (term + 1) * states] = value.T
-
-        owner = sec * slots + t
+        for n in range(len(blocks)):
+            for t in range(terms):
+                store(n, t, out[n * states : (n + 1) * states, t * block : (t + 1) * block].astype(BF16))
+
+    def own_slot(t, carry):
+        def store(n, term, value):
+            own_ref[t, n * block : (n + 1) * block, term * states : (term + 1) * states] = value.T
+
         gate_left(
-            [lown[t, pl.ds(first, block), :]], [row * rows + first], live_ref[owner] * site, store
+            [
+                [(lown[t, first : first + block, :], row * rows + first)]
+                for first in range(0, rows, block)
+            ],
+            live_ref[sec * slots + t] * site, store,
         )
         return carry
 
-    lax.fori_loop(0, slots * (rows // block), own_chunk, 0)
+    lax.fori_loop(0, slots, own_slot, 0)
 
     limit = live_ref[mirror] * site
     forwarded = []
@@ -336,25 +338,27 @@
                 owners.append(owner)
         return owners
 
-    def gate_pieces(owners, k, column):
-        for index in range(0, len(owners), ready):
-            firsts = [owner * rows + k * piece for owner in owners[index : index + ready]]
-            place = column + index * piece
-
-            def store(t, value):
-                at_ref[t * states : (t + 1) * states, place : place + block] = value
-
-            gate_left(
-                [lrecv[pl.ds(pl.multiple_of(first, piece), piece), :] for first in firsts],
-                firsts, limit, store,
-            )
+    def blocks_of(owners, k):
+        firsts = [owner * rows + k * piece for owner in owners]
+        parts = [(lrecv[pl.ds(pl.multiple_of(first, piece), piece), :], first) for first in firsts]
+        return [parts[index : index + ready] for index in range(0, len(parts), ready)]
 
     gram = None
     for k in range(PIECES + 1):
+        blocks, places = [], []
         if k < PIECES:
-            gate_pieces(arrive(k), k, k * span)
+            blocks = blocks_of(arrive(k), k)
+            places = [k * span + n * block for n in range(len(blocks))]
         if k:
-            gate_pieces(arrive_from_mates(k - 1), k - 1, (k - 1) * span + slots * piece)
+            late = blocks_of(arrive_from_mates(k - 1), k - 1)
+            blocks = blocks + late
+            places += [(k - 1) * span + slots * piece + n * block for n in range(len(late))]
+
+        def store(n, t, value):
+            at_ref[t * states : (t + 1) * states, places[n] : places[n] + block] = value
+
+        gate_left(blocks, limit, store)
+        if k:
             done = at_ref[:, (k - 1) * span : k * span]
             gram = nt(done, done) if gram is None else ga_ref[...] + nt(done, done)
             if k < PIECES:

time: 42.9 us -> 42.7 us (level)
  no operation moved by 1% of the time
where the time goes in v8:
time: 42.7 us; the launch traced here: 42.6 us
  Pallas kernels  40.3 us (94%)
  local copies, waits for them, and re-layouts  1.59 us (4%)
  between operations  0.64 us (1%)
    pallas_call x1, Pallas kernels, on_device(): pl.pallas_call(functools.partial(gate_kernel, row_count, sec_count), out_...  40.3 us
    unnamed x2, local copies, waits for them, and re-layouts  1.59 us

profile of v8, /device:TPU:0, one launch (start us, length us, event | category | flops | bytes accessed | tf_op | source)
XLA Modules:
  0.0 42.6 jit_solution(1806365849659759149)
XLA Ops:
  0.6 40.3 %shard_map.95 = (f32[2,512,128]{2,1,0:T(8,128)S(1)}, f32[2,128,512]{2,1,0:T(8,128)S(1)}) custom-call(bf16[2,512,128]{2,1,0:T(8,128)(2,1)} %left_hbm.1, bf16[2,128,2048]{2,1,0:T(8,128)(2,1)} %right_hbm.1, f32[4,16,16]{2,1,0:T(8,128)} %lops_hbm.1, f32[4,16,16]{2,1,0:T(8,128)} %rops_hbm.1, s32[16]{0:T(128)} %charges_hbm.1, s32[16]{0:T(128)} %live_hbm.1, ...), custom_call_target="tpu_custom_call" | custom-call | tf_op jit(solution)/shard_map/pallas_call | solution.py:557
  41.0 0.8 %copy.12 = f32[2,512,128]{2,1,0:T(8,128)} copy(f32[2,512,128]{2,1,0:T(8,128)S(1)} %get-tuple-element.2) | data formatting | bytes 1048576
  41.8 0.8 %copy.13 = f32[2,128,512]{2,1,0:T(8,128)} copy(f32[2,128,512]{2,1,0:T(8,128)S(1)} %get-tuple-element.3) | data formatting | bytes 1048576

commit v9 on v8

--- a/solution.py
+++ b/solution.py
@@ -582,7 +582,7 @@
                 pltpu.VMEM((bond, bond), BF16),
                 pltpu.VMEM((keep, keep), F32),
                 pltpu.VMEM((keep, keep), F32),
-                pltpu.VMEM((RING, 2, PANEL, keep), F32),
+                pltpu.VMEM((RING, 2, PANEL + TILE, keep), F32),
                 pltpu.VMEM((bond, keep), F32),
                 pltpu.VMEM((bond // mates, keep), BF16),
                 pltpu.VMEM((slots, bond, keep), BF16),

time: 42.7 us -> 42.7 us (level)
  no operation moved by 1% of the time
where the time goes in v9:
time: 42.7 us; the launch traced here: 42.5 us
  Pallas kernels  40.3 us (94%)
  local copies, waits for them, and re-layouts  1.59 us (4%)
  between operations  0.64 us (1%)
    pallas_call x1, Pallas kernels, on_device(): pl.pallas_call(functools.partial(gate_kernel, row_count, sec_count), out_...  40.3 us
    unnamed x2, local copies, waits for them, and re-layouts  1.59 us

profile of v9, /device:TPU:0, one launch (start us, length us, event | category | flops | bytes accessed | tf_op | source)
XLA Modules:
  0.0 42.5 jit_solution(1191585835054831642)
XLA Ops:
  0.6 40.3 %shard_map.95 = (f32[2,512,128]{2,1,0:T(8,128)S(1)}, f32[2,128,512]{2,1,0:T(8,128)S(1)}) custom-call(bf16[2,512,128]{2,1,0:T(8,128)(2,1)} %left_hbm.1, bf16[2,128,2048]{2,1,0:T(8,128)(2,1)} %right_hbm.1, f32[4,16,16]{2,1,0:T(8,128)} %lops_hbm.1, f32[4,16,16]{2,1,0:T(8,128)} %rops_hbm.1, s32[16]{0:T(128)} %charges_hbm.1, s32[16]{0:T(128)} %live_hbm.1, ...), custom_call_target="tpu_custom_call" | custom-call | tf_op jit(solution)/shard_map/pallas_call | solution.py:557
  41.0 0.8 %copy.12 = f32[2,512,128]{2,1,0:T(8,128)} copy(f32[2,512,128]{2,1,0:T(8,128)S(1)} %get-tuple-element.2) | data formatting | bytes 1048576
  41.8 0.8 %copy.13 = f32[2,128,512]{2,1,0:T(8,128)} copy(f32[2,128,512]{2,1,0:T(8,128)S(1)} %get-tuple-element.3) | data formatting | bytes 1048576
